TPU v7x, 128 devices: a whole 4x4x4 slice. The times are simulated.
128 devices in a mesh: gx: 8 (over x, core), gy: 16 (over z, y).
Axes of the slice: x: 4, y: 4, z: 4, core: 2. Of those that a mesh axis runs over, the one named last changes fastest.
Arguments:
- samples: float32 [16384, 2, 128], P(('gx', 'gy')), may hold values from -6 to 6
- kernel: float32 [16384, 3, 4, 128], P(('gx', 'gy')), may hold values from 0.1 to 1
- offsets: int32 [16384, 3, 128], P(('gx', 'gy')), may hold values from 0 to 4
- owners: int32 [16384, 1], P(('gx', 'gy')), may hold values from 0 to 127; in each aligned block of 128 rows (0 to 127, 128 to 255, ...) at most 2 rows name the same one
- tile_ids: int32 [16384], P(('gx', 'gy')), may hold values from 0 to 863
- deapod_first: float32 [192], replicated, may hold values from 1 to 3
- deapod_second: float32 [192], P('gx'), may hold values from 1 to 3
- deapod_third: float32 [192], P('gy'), may hold values from 1 to 3
Outputs:
- image: float32 [2, 192, 192, 192], P(None, 'gy', 'gx')
Inputs may be any that keep to these rules, and one draw needn't show every extreme that they name: `owners`: among the 128 blocks of one device no owner is named more than 2 times, and in some device one owner is named exactly 2 times. `tile_ids`: tiles are numbered row, column, depth over the owner's 6 x 3 x 48 tiles. `offsets`: each sample's kernel lies inside its block's tile.
All inputs are finite; a program needn't handle non-finite values.
Results may differ from a plain program's by a relative error of at most 0.0003.
Values sent between devices are 32-bit elements; how exact they have to be, the bound alone decides.
A program may use at most 128 MiB of HBM per device.

v0:
```python
import math

import jax
import jax.numpy as jnp
from jax import lax
from jax.sharding import PartitionSpec as P

NX = 384
NY = 384
NZ = 384
TILE = 8


def fourier_table(length, outputs):
    freq = jnp.arange(length, dtype=jnp.int32) - length // 2
    image_pos = jnp.arange(outputs, dtype=jnp.int32) - outputs // 2
    phase_steps = jnp.mod(freq[:, None] * image_pos[None, :], length)
    phases = phase_steps.astype(jnp.float32) * (2.0 * math.pi / length)
    norming = 1.0 / math.sqrt(length)
    return (jnp.cos(phases) * norming, jnp.sin(phases) * norming)


def complex_apply(real_part, imag_part, cos_table, sin_table, pattern):
    highest = lax.Precision.HIGHEST
    real_cos = jnp.einsum(pattern, real_part, cos_table, precision=highest)
    real_sin = jnp.einsum(pattern, real_part, sin_table, precision=highest)
    imag_cos = jnp.einsum(pattern, imag_part, cos_table, precision=highest)
    imag_sin = jnp.einsum(pattern, imag_part, sin_table, precision=highest)
    return jnp.stack((real_cos - imag_sin, real_sin + imag_cos))


def spread(values, kernel, starts, tile_width):
    kernel_taps = jnp.arange(kernel.shape[2], dtype=jnp.float32)
    cell_axis = jnp.arange(tile_width, dtype=jnp.float32)
    matches = (
        cell_axis[None, None, :, None, None]
        == starts[:, :, None, None, :] + kernel_taps[None, None, None, :, None]
    ).astype(jnp.float32)
    placed = jnp.sum(matches * kernel[:, :, None, :, :], axis=3)
    plane_weight = placed[:, 0][:, :, None, :] * placed[:, 1][:, None, :, :]
    depth_weight = values[:, :, None, :] * placed[:, 2][:, None, :, :]
    return jnp.einsum(
        "nijs,ncls->ncijl", plane_weight, depth_weight, precision=lax.Precision.HIGHEST
    )


def on_device(
    samples, kernel, offsets, owners, tile_ids, deapod_first, deapod_second, deapod_third
):
    devices = lax.axis_size(("gx", "gy"))
    grid_rows = lax.axis_size("gx")
    grid_cols = lax.axis_size("gy")
    blocks = samples.shape[0]
    block_width = samples.shape[2]
    kernel_taps = kernel.shape[2]
    capacity = max(2, 2 * blocks // devices)
    tile_rows = NX // (TILE * grid_rows)
    tile_cols = NY // (TILE * grid_cols)
    tile_depth = NZ // TILE
    tile_count = tile_rows * tile_cols * tile_depth
    starts = offsets.astype(jnp.float32)
    target = owners[:, 0]
    onehot = (target[:, None] == jnp.arange(devices, dtype=jnp.int32)[None, :]).astype(jnp.float32)
    earlier = (jnp.arange(blocks)[:, None] > jnp.arange(blocks)[None, :]).astype(jnp.float32)
    counted = jnp.dot(earlier, onehot, precision=lax.Precision.HIGHEST)
    position = jnp.sum(counted * onehot, axis=1).astype(jnp.int32)
    marker = jnp.broadcast_to(tile_ids.astype(jnp.float32)[:, None, None], (blocks, 1, block_width))
    payload = jnp.concatenate(
        (samples, kernel.reshape(blocks, 3 * kernel_taps, block_width), starts, marker), axis=1
    )
    payload_rows = payload.shape[1]
    outbox = jnp.zeros((devices, capacity, payload_rows, block_width), jnp.float32)
    outbox = outbox.at[:, :, payload_rows - 1, :].set(float(tile_count))
    outbox = outbox.at[target, position].set(payload)
    arrived = lax.all_to_all(outbox, ("gx", "gy"), split_axis=0, concat_axis=0, tiled=True)
    arrived = arrived.reshape(devices * capacity, payload_rows, block_width)
    tile_index = arrived[:, payload_rows - 1, 0].astype(jnp.int32)
    pieces = spread(
        arrived[:, 0:2],
        arrived[:, 2 : 2 + 3 * kernel_taps].reshape(-1, 3, kernel_taps, block_width),
        arrived[:, 2 + 3 * kernel_taps : 5 + 3 * kernel_taps],
        TILE,
    )
    cos_z, sin_z = fourier_table(NZ, NZ // 2)
    tile_cells = 2 * TILE * TILE * TILE
    flat_pieces = pieces.reshape(-1, tile_cells)
    spread_grid = (
        jnp.zeros((tile_count, tile_cells), jnp.float32)
        .at[tile_index]
        .add(flat_pieces, mode="drop")
    )
    spread_grid = (
        spread_grid.reshape(tile_rows, tile_cols, tile_depth, 2, TILE, TILE, TILE)
        .transpose(3, 0, 4, 1, 5, 2, 6)
        .reshape(2, tile_rows * TILE, tile_cols * TILE, NZ)
    )
    along_z = complex_apply(spread_grid[0], spread_grid[1], cos_z, sin_z, "xyk,km->mxy")
    cos_y, sin_y = fourier_table(NY, NY // 2)
    slab = lax.all_to_all(along_z, "gy", split_axis=1, concat_axis=3, tiled=True)
    along_y = complex_apply(slab[0], slab[1], cos_y, sin_y, "zxy,yq->zqx")
    cos_x, sin_x = fourier_table(NX, NX // 2)
    slab = lax.all_to_all(along_y, "gx", split_axis=2, concat_axis=3, tiled=True)
    along_x = complex_apply(slab[0], slab[1], cos_x, sin_x, "zyx,xp->zyp")
    return (
        along_x
        * deapod_third[None, :, None, None]
        * deapod_second[None, None, :, None]
        * deapod_first[None, None, None, :]
    )


def solution(mesh):
    in_specs = (
        P(("gx", "gy"), None, None),
        P(("gx", "gy"), None, None, None),
        P(("gx", "gy"), None, None),
        P(("gx", "gy"), None),
        P(("gx", "gy")),
        P(),
        P("gx"),
        P("gy"),
    )
    out_specs = P(None, "gy", "gx", None)
    return jax.shard_map(
        on_device, mesh=mesh, in_specs=in_specs, out_specs=out_specs, check_vma=False
    )
```

profile of v0, /device:TPU:1, one launch (start us, length us, event | category | flops | bytes accessed | tf_op | source)
XLA Modules:
  0.0 435.6 jit_solution(14380070019830126358)
XLA Ops:
  7.7 13.1 %scatter_fusion = f32[128,2,18,128]{3,2,1,0:T(8,128)S(1)} fusion(f32[128,2,18,128]{3,2,1,0:T(8,128)S(1)} %copy-done, s32[128]{0:T(128)S(1)} %fusion.105, f32[128,18,128]{2,1,0:T(8,128)} %copy.121), kind=kCustom, calls=%fused_computation | custom fusion | bytes 3539968 | tf_op jit(solution)/shard_map/scatter | solution.py:74
  23.4 11.5 %all-to-all-start = ((f32[128,2,18,128]{3,1,2,0:T(2,128)}), f32[128,2,18,128]{3,1,2,0:T(2,128)S(1)}, u32[]{:S(2)}, u32[]{:S(2)}) async-start(f32[128,2,18,128]{3,1,2,0:T(2,128)} %copy.122), calls=%async_computation | async-start | bytes 4718592 | tf_op jit(solution)/shard_map/all_to_all | solution.py:75
  34.9 31.9 %all-to-all-done = f32[128,2,18,128]{3,1,2,0:T(2,128)S(1)} async-done(((f32[128,2,18,128]{3,1,2,0:T(2,128)}), f32[128,2,18,128]{3,1,2,0:T(2,128)S(1)}, u32[]{:S(2)}, u32[]{:S(2)}) %all-to-all-start) | async-done | bytes 2359328 | tf_op jit(solution)/shard_map/all_to_all | solution.py:75
  70.0 2.7 select_reduce_fusion
  73.2 114.2 %convolution_bitcast_fusion = f32[256,2,8,8,8]{3,4,2,1,0:T(8,128)} fusion(f32[256,8,128]{2,1,0:T(8,128)S(1)} %get-tuple-element.22, f32[256,8,128]{2,1,0:T(8,128)S(1)} %get-tuple-element.23, f32[256,8,128]{2,1,0:T(8,128)S(1)} %get-tuple-element.21, f32[256,2,128]{2,1,0:T(2,128)S(1)} %copy.124), kind=kOutput, calls=%fused_computation.4 | convolution fusion | flops 405274624 | bytes 4456448 | tf_op jit(solution)/shard_map/nijs,ncls->ncijl/dot_general | solution.py:42
  187.4 11.9 %copy.127 = f32[256,2,8,8,8]{0,4,3,2,1:T(8,128)S(1)} copy(f32[256,2,8,8,8]{3,4,2,1,0:T(8,128)} %convolution_bitcast_fusion) | data formatting | bytes 2097152 | tf_op jit(solution)/shard_map/nijs,ncls->ncijl/transpose | solution.py:42
  200.6 4.2 scatter_custom_fusion.1
  204.8 3.4 copy.129
  208.2 13.5 %reshape.122 = f32[6,3,48,2,8,8,8]{2,1,0,6,5,4,3:T(4,128)} reshape(f32[864,1024]{0,1:T(8,128)} %copy.129) | data formatting | bytes 7077888 | tf_op jit(solution)/shard_map/reshape | solution.py:93
  221.7 13.8 %fusion.154 = (f32[1,6,8,3,8,48,8]{5,3,1,6,4,2,0:T(4,128)}, f32[1,6,8,3,8,48,8]{5,3,1,6,4,2,0:T(4,128)}) fusion(f32[2,6,8,3,8,48,8]{5,3,1,6,4,2,0:T(4,128)} %bitcast.112), kind=kLoop, calls=%fused_computation.177 | loop fusion | bytes 7077888 | tf_op jit(solution)/shard_map/slice | solution.py:97
  235.5 18.1 %copy.154 = f32[1,6,8,3,8,48,8]{6,5,2,1,4,3,0:T(8,128)} copy(f32[1,6,8,3,8,48,8]{5,3,1,6,4,2,0:T(4,128)} %get-tuple-element.18) | data formatting | bytes 3538944 | tf_op jit(solution)/shard_map/squeeze | solution.py:97
  253.6 19.6 %reshape.141 = f32[48,24,384]{2,0,1:T(8,128)S(1)} reshape(f32[1,6,8,3,8,48,8]{6,5,2,1,4,3,0:T(8,128)} %copy.154) | data formatting | bytes 3538944 | tf_op jit(solution)/shard_map/squeeze | solution.py:97
  273.2 4.2 fusion.37
  277.4 3.2 fusion.27
  280.6 18.1 %copy.155 = f32[1,6,8,3,8,48,8]{6,5,2,1,4,3,0:T(8,128)} copy(f32[1,6,8,3,8,48,8]{5,3,1,6,4,2,0:T(4,128)} %get-tuple-element.17) | data formatting | bytes 3538944 | tf_op jit(solution)/shard_map/squeeze | solution.py:97
  298.7 19.3 %reshape.142 = f32[48,24,384]{2,0,1:T(8,128)S(1)} reshape(f32[1,6,8,3,8,48,8]{6,5,2,1,4,3,0:T(8,128)} %copy.155) | data formatting | bytes 3538944 | tf_op jit(solution)/shard_map/squeeze | solution.py:97
  318.0 4.5 %fusion.9 = f32[1,192,48,24]{1,2,3,0:T(8,128)S(1)} fusion(f32[192,48,24]{0,1,2:T(8,128)} %fusion.37, f32[48,24,384]{2,0,1:T(8,128)S(1)} %reshape.142, s32[192]{0:T(256)S(1)} %iota_add_fusion.2, s32[384]{0:T(512)S(1)} %iota_add_fusion.1), kind=kOutput, calls=%fused_computation.18 | convolution fusion | flops 1020174336 | bytes 3541248 | tf_op jit(solution)/shard_map/xyk,km->mxy/dot_general | solution.py:28
  322.5 3.2 fusion.8
  325.9 4.1 copy.136
  330.0 6.0 %reshape.146 = f32[16,1,27648]{2,1,0:T(1,128)S(1)} reshape(f32[192,2,24,48]{3,2,1,0:T(8,128)} %bitcast.118) | data formatting | bytes 3538944
  336.0 27.9 %all_to_all.35 = f32[16,1,27648]{2,1,0:T(1,128)S(1)} all-to-all(f32[16,1,27648]{2,1,0:T(1,128)S(1)} %reshape.146), channel_id=1, replica_groups=mesh['gx'=8,'gy'=16] {'gy'}, dimensions={0} | all-to-all | bytes 3538944 | tf_op jit(solution)/shard_map/all_to_all | solution.py:99
  364.4 4.9 %reduce.4 = f32[16,27648]{1,0:T(8,128)S(1)} reduce(f32[16,1,27648]{2,1,0:T(1,128)S(1)} %all_to_all.35, f32[]{:T(128)} %broadcast.236), dimensions={1}, to_apply=%all_to_all.26.reduce_sub_computation | reduce | bytes 3538948 | tf_op jit(solution)/shard_map/all_to_all | solution.py:99
  369.3 3.8 reshape.147
  373.1 2.6 copy.137
  376.2 4.7 %fusion.34 = f32[192,12,48]{0,2,1:T(8,128)S(1)} fusion(f32[12,48,384]{1,2,0:T(8,128)S(1)} %bitcast.115, s32[192]{0:T(256)S(1)} %iota_add_fusion.2, s32[384]{0:T(512)S(1)} %iota_add_fusion.1), kind=kOutput, calls=%fused_computation.55 | convolution fusion | flops 510345216 | bytes 1329408 | tf_op jit(solution)/shard_map/zxy,yq->zqx/dot_general | solution.py:25
  381.0 4.7 %fusion.24 = f32[192,12,48]{0,2,1:T(8,128)S(1)} fusion(f32[12,48,384]{1,2,0:T(8,128)S(1)} %bitcast.116, s32[192]{0:T(256)S(1)} %iota_add_fusion.2, s32[384]{0:T(512)S(1)} %iota_add_fusion.1), kind=kOutput, calls=%fused_computation.45 | convolution fusion | flops 510345216 | bytes 1329408 | tf_op jit(solution)/shard_map/zxy,yq->zqx/dot_general | solution.py:26
  385.9 4.9 %fusion.11 = f32[1,12,192,48]{2,3,1,0:T(8,128)S(1)} fusion(f32[192,12,48]{0,2,1:T(8,128)S(1)} %fusion.34, f32[12,48,384]{1,2,0:T(8,128)S(1)} %bitcast.113, s32[192]{0:T(256)S(1)} %iota_add_fusion.2, s32[384]{0:T(512)S(1)} %iota_add_fusion.1), kind=kOutput, calls=%fused_computation.22 | convolution fusion | flops 510455808 | bytes 1771776 | tf_op jit(solution)/shard_map/zxy,yq->zqx/dot_general | solution.py:28
  390.8 4.7 %fusion.10 = f32[1,12,192,48]{2,3,1,0:T(8,128)S(1)} fusion(f32[192,12,48]{0,2,1:T(8,128)S(1)} %fusion.24, f32[12,48,384]{1,2,0:T(8,128)S(1)} %bitcast.114, s32[192]{0:T(256)S(1)} %iota_add_fusion.2, s32[384]{0:T(512)S(1)} %iota_add_fusion.1), kind=kOutput, calls=%fused_computation.20 | convolution fusion | flops 510455808 | bytes 1771776 | tf_op jit(solution)/shard_map/zxy,yq->zqx/dot_general | solution.py:27
  397.2 3.9 reshape.148
  401.1 17.6 %all_to_all.36 = f32[8,1,27648]{2,1,0:T(1,128)S(1)} all-to-all(f32[8,1,27648]{2,1,0:T(1,128)S(1)} %reshape.148), channel_id=1, replica_groups=mesh['gx'=8,'gy'=16] {'gx'}, dimensions={0} | all-to-all | bytes 1769472 | tf_op jit(solution)/shard_map/all_to_all | solution.py:102
  418.7 2.7 reduce.5
  421.5 3.8 reshape.149
  (52 shorter events, 28.0 us)
Async XLA Ops:
  5.8 0.7 copy-start.4
  5.8 1.9 copy-start
  23.4 43.4 %all-to-all-start = ((f32[128,2,18,128]{3,1,2,0:T(2,128)}), f32[128,2,18,128]{3,1,2,0:T(2,128)S(1)}, u32[]{:S(2)}, u32[]{:S(2)}) async-start(f32[128,2,18,128]{3,1,2,0:T(2,128)} %copy.122), calls=%async_computation | async-start | bytes 4718592 | tf_op jit(solution)/shard_map/all_to_all | solution.py:75
  430.3 4.0 copy-start.1
  430.3 4.0 copy-start.2
  430.4 4.0 copy-start.3
where the time goes:
time: 444 us; the launch traced here: 436 us
  local copies, waits for them, and re-layouts  172 us (39%)
  matrix products  156 us (35%)
  blocking collectives  45.6 us (10%)
  waiting for transfers between devices  31.9 us (7%)
  other arithmetic  17.9 us (4%)
  starting transfers between devices  11.5 us (3%)
    dot_general x1, matrix products, spread(): jnp.einsum('nijs,ncls->ncijl', plane_weight, depth_weight, precision=lax....  114 us
    squeeze x2, local copies, waits for them, and re-layouts, on_device(): spread_grid[0]  37.7 us
    squeeze x2, local copies, waits for them, and re-layouts, on_device(): spread_grid[1]  37.4 us
    all_to_all x1, waiting for transfers between devices, on_device(): lax.all_to_all(outbox, ('gx', 'gy'), split_axis=0, concat_axis=0, tiled=T...  31.9 us
    all_to_all x1, blocking collectives, on_device(): lax.all_to_all(along_z, 'gy', split_axis=1, concat_axis=3, tiled=True)  27.9 us
    unnamed x16, local copies, waits for them, and re-layouts  21.3 us
    all_to_all x1, blocking collectives, on_device(): lax.all_to_all(along_y, 'gx', split_axis=2, concat_axis=3, tiled=True)  17.6 us
    scatter x2, local copies, waits for them, and re-layouts, on_device(): outbox = outbox.at[target, position].set(payload)  15.7 us
  transfers between devices with their start and end apart: 1, of which 1 were waited for; matrix products, arithmetic and copies ran while one was open for 0% of the time, Pallas kernels for 0%

commit v1 on v0

v1 whole, which is shorter than its diff:
```python
import math

import jax
import jax.numpy as jnp
import ml_dtypes
import numpy as np
from jax import lax
from jax.experimental import pallas as pl
from jax.experimental.pallas import tpu as pltpu
from jax.sharding import PartitionSpec as P

N = 384
M = 192
DEVICES = 128
ROWS, COLS = 8, 16
BLOCKS = 128
TILES = 864
SLOT_ROWS = 17
ROUNDS = 3
MESH = pl.DeviceIdType.MESH
F32 = jnp.float32
BF16 = jnp.bfloat16


def angles(cells, images):
    steps = np.mod((cells[:, None] - N // 2) * (images[None, :] - M // 2), N)
    phases = steps.astype(np.float64) * (2.0 * math.pi / N)
    return np.cos(phases) / math.sqrt(N), np.sin(phases) / math.sqrt(N)


def halves(table):
    table = table.astype(np.float32)
    high = table.astype(ml_dtypes.bfloat16)
    low = (table - high.astype(np.float32)).astype(ml_dtypes.bfloat16)
    return high, low


def left_table(cells, images):
    cos, sin = angles(cells, images)
    high, low = halves(np.concatenate((cos.T, sin.T)))
    return np.concatenate((high, low, high), axis=1)


def tables():
    every = np.arange(M)
    a, pair, side, low = np.meshgrid(np.arange(3), np.arange(8), np.arange(2), np.arange(4), indexing="ij")
    order = (12 * (2 * pair + side) + 4 * a + low).reshape(-1)
    third = left_table(np.arange(N), order)
    q, g, j = np.meshgrid(np.arange(3), np.arange(COLS), np.arange(8), indexing="ij")
    second = left_table((g * 24 + q * 8 + j).reshape(-1), every)
    turn, lane = np.meshgrid(np.arange(ROUNDS), np.arange(128), indexing="ij")
    source = (lane >> 6) * 4 + (lane & 3)
    cells = source * 48 + (2 * turn + ((lane >> 2) & 1)) * 8 + ((lane >> 3) & 7)
    firsts = []
    for part in angles(cells.reshape(-1), every):
        high, low = halves(part)
        firsts.append(np.concatenate((high, low, high), axis=0))
    return third, second, firsts[0], firsts[1]


def split(value):
    high = value.astype(BF16)
    return high, (value - high.astype(F32)).astype(BF16)


def exchange_bit(value, axis_low, lane_bit):
    count, rows, lanes = value.shape
    shift = 1 << lane_bit
    pairs = value.reshape(count // (2 * axis_low), 2, axis_low * rows, lanes)
    first = pairs[:, 0].reshape(-1, lanes)
    second = pairs[:, 1].reshape(-1, lanes)
    lane = lax.broadcasted_iota(jnp.int32, first.shape, 1)
    upper = (lane & shift) != 0
    new_first = jnp.where(upper, pltpu.roll(second, shift, 1), first)
    new_second = jnp.where(upper, second, pltpu.roll(first, lanes - shift, 1))
    shape = (count // (2 * axis_low), axis_low * rows, lanes)
    out = jnp.stack((new_first.reshape(shape), new_second.reshape(shape)), axis=1)
    return out.reshape(value.shape)


def combine(product):
    rows = product.shape[0] // 2
    lane = lax.broadcasted_iota(jnp.int32, (rows, 128), 1)
    turned = pltpu.roll(product[rows:], 64, 1)
    return product[:rows] + jnp.where(lane < 64, -turned, turned)


NT = (((1,), (1,)), ((), ()))


def spread_kernel(owners, tile_ids, samples, kernel, offsets, out, table):
    out[...] = jnp.zeros_like(out)

    @pl.loop(0, DEVICES)
    def _(d):
        table[0, d] = TILES
        table[1, d] = TILES

    cell = lax.broadcasted_iota(jnp.int32, (8, 128), 0)

    def place(n, dim):
        away = cell - offsets[n, pl.ds(dim, 1), :]
        total = jnp.zeros((8, 128), F32)
        for k in range(4):
            total = jnp.where(away == k, kernel[n, dim, pl.ds(k, 1), :], total)
        return total

    def one(n):
        first, second, third = place(n, 0), place(n, 1), place(n, 2)
        real = samples[n, pl.ds(0, 1), :] * first
        imag = samples[n, pl.ds(1, 1), :] * first
        plane = jnp.concatenate((real, imag), axis=0)
        weight = (plane[:, None, :] * second[None, :, :]).reshape(128, 128)
        high, low = split(weight)
        depth_high, depth_low = split(third)
        left = jnp.concatenate(
            (
                jnp.concatenate((depth_high, depth_high), axis=1),
                jnp.concatenate((depth_low, jnp.zeros_like(depth_low)), axis=1),
            ),
            axis=0,
        )
        right = jnp.concatenate((high, low), axis=1)
        both = lax.dot_general(left, right, NT, preferred_element_type=F32)
        piece = both[:8] + both[8:]
        dest = owners[n]
        seen = (table[0, dest] != TILES).astype(jnp.int32)
        table[seen, dest] = tile_ids[n]
        out[dest, pl.ds(pl.multiple_of(seen * 8, 8), 8), :] = piece

    @pl.loop(0, BLOCKS // 4)
    def _(step):
        for u in range(4):
            one(step * 4 + u)

    lane = lax.broadcasted_iota(jnp.int32, (1, 128), 1)

    @pl.loop(0, DEVICES)
    def _(d):
        out[d, pl.ds(16, 1), :] = jnp.where(lane < 64, table[0, d], table[1, d]).astype(F32)


def spread(owners, tile_ids, samples, kernel, offsets):
    vmem = pl.BlockSpec(memory_space=pltpu.VMEM)
    smem = pl.BlockSpec(memory_space=pltpu.SMEM)
    return pl.pallas_call(
        spread_kernel,
        out_shape=jax.ShapeDtypeStruct((DEVICES, SLOT_ROWS, 128), F32),
        in_specs=[smem, smem, vmem, vmem, vmem],
        out_specs=vmem,
        scratch_shapes=[pltpu.SMEM((2, DEVICES), jnp.int32)],
        compiler_params=pltpu.CompilerParams(vmem_limit_bytes=32 << 20),
        name="spread",
    )(owners, tile_ids, samples, kernel, offsets)


def route_kernel(x, out, send_sem, recv_sem, local_sem):
    gx, gy = lax.axis_index("gx"), lax.axis_index("gy")
    me = gx * COLS + gy
    own = pltpu.make_async_copy(x.at[me], out.at[me], local_sem)
    own.start()

    def copy(peer, lands):
        return pltpu.make_async_remote_copy(
            src_ref=x.at[peer],
            dst_ref=out.at[lands],
            send_sem=send_sem.at[peer],
            recv_sem=recv_sem.at[lands],
            device_id=(peer // COLS, lax.rem(peer, COLS)),
            device_id_type=MESH,
        )

    @pl.loop(1, DEVICES)
    def _(k):
        copy(lax.rem(me + k, DEVICES), me).start()

    own.wait()

    @pl.loop(1, DEVICES)
    def _(k):
        peer = lax.rem(me + DEVICES - k, DEVICES)
        copy(peer, peer).wait_recv()

    @pl.loop(1, DEVICES)
    def _(k):
        peer = lax.rem(me + k, DEVICES)
        copy(peer, me).wait_send()


def route(outbox):
    return pl.pallas_call(
        route_kernel,
        out_shape=jax.ShapeDtypeStruct(outbox.shape, outbox.dtype),
        in_specs=[pl.BlockSpec(memory_space=pltpu.VMEM)],
        out_specs=pl.BlockSpec(memory_space=pltpu.VMEM),
        scratch_shapes=[
            pltpu.SemaphoreType.DMA((DEVICES,)),
            pltpu.SemaphoreType.DMA((DEVICES,)),
            pltpu.SemaphoreType.DMA,
        ],
        compiler_params=pltpu.CompilerParams(has_side_effects=True, vmem_limit_bytes=32 << 20),
        name="route",
    )(outbox)


def gather_kernel(inbox, grid, ids, slots, sem):
    marks = inbox[:, 16, :]
    lane = lax.broadcasted_iota(jnp.int32, (DEVICES, 128), 1)
    source = lax.broadcasted_iota(jnp.int32, (DEVICES, 128), 0)
    marks = jnp.where((lane & 63) == (source & 63), marks, 0.0)
    ids[pl.ds(0, 1), :] = jnp.sum(marks[:64], axis=0, keepdims=True).astype(jnp.int32)
    ids[pl.ds(1, 1), :] = jnp.sum(marks[64:], axis=0, keepdims=True).astype(jnp.int32)
    copy = pltpu.make_async_copy(ids, slots, sem)
    copy.start()
    grid[...] = jnp.zeros_like(grid)
    copy.wait()
    for half in range(2):

        @pl.loop(0, 64 // 4)
        def _(step):
            for u in range(4):
                s = step * 4 + u
                for slot in range(2):
                    t = slots[half, slot * 64 + s]
                    grid[t] = grid[t] + inbox[half * 64 + s, pl.ds(slot * 8, 8), :]


def gather(inbox):
    vmem = pl.BlockSpec(memory_space=pltpu.VMEM)
    return pl.pallas_call(
        gather_kernel,
        out_shape=jax.ShapeDtypeStruct((TILES + 1, 8, 128), F32),
        in_specs=[vmem],
        out_specs=vmem,
        scratch_shapes=[
            pltpu.VMEM((8, 128), jnp.int32),
            pltpu.SMEM((8, 128), jnp.int32),
            pltpu.SemaphoreType.DMA,
        ],
        compiler_params=pltpu.CompilerParams(vmem_limit_bytes=32 << 20),
        name="gather",
    )(inbox)


def transform_kernel(
    grid,
    third,
    second,
    first_cos,
    first_sin,
    out,
    out_z,
    in_y,
    rows_y,
    out_y,
    in_x,
    rows_x,
    z_send,
    z_recv,
    y_send,
    y_recv,
    own_sem,
):
    gx, gy = lax.axis_index("gx"), lax.axis_index("gy")

    def send_z(turn, peer, lands):
        return pltpu.make_async_remote_copy(
            src_ref=out_z.at[turn, peer // 2, lax.rem(peer, 2)],
            dst_ref=in_y.at[turn, lands],
            send_sem=z_send.at[turn, peer],
            recv_sem=z_recv.at[turn, lands],
            device_id=(gx, peer),
            device_id_type=MESH,
        )

    def own_z(turn):
        return pltpu.make_async_copy(
            out_z.at[turn, gy // 2, lax.rem(gy, 2)], in_y.at[turn, gy], own_sem.at[0, turn]
        )

    def send_y(turn, peer, lands):
        return pltpu.make_async_remote_copy(
            src_ref=out_y.at[turn, peer],
            dst_ref=in_x.at[turn, lands],
            send_sem=y_send.at[turn, peer],
            recv_sem=y_recv.at[turn, lands],
            device_id=(peer, gy),
            device_id_type=MESH,
        )

    def own_y(turn):
        return pltpu.make_async_copy(out_y.at[turn, gx], in_x.at[turn, gx], own_sem.at[1, turn])

    row = lax.broadcasted_iota(jnp.int32, (24, 8, 128), 1)
    for turn in range(ROUNDS):
        for q in range(3):
            cells = jnp.concatenate(
                [
                    grid[pl.ds(((2 * turn + r) * 3 + q) * 48, 48)].reshape(N, 128)
                    for r in range(2)
                ],
                axis=1,
            )
            high, low = split(cells)
            product = jnp.dot(
                third[...], jnp.concatenate((high, high, low), axis=0), preferred_element_type=F32
            )
            near = combine(product[:, :128]).reshape(24, 8, 128)
            far = combine(product[:, 128:]).reshape(24, 8, 128)
            even = jnp.where(row < 4, near, pltpu.roll(far, 4, 1))
            odd = jnp.where(row < 4, pltpu.roll(near, 4, 1), far)
            for a in range(3):
                out_z[turn, :, 0, q * 3 + a] = even[a * 8 : a * 8 + 8]
                out_z[turn, :, 1, q * 3 + a] = odd[a * 8 : a * 8 + 8]
        own_z(turn).start()

        @pl.loop(1, COLS)
        def _(k):
            send_z(turn, lax.rem(gy + k, COLS), gy).start()

    for turn in range(ROUNDS):
        own_z(turn).wait()

        @pl.loop(1, COLS)
        def _(k):
            peer = lax.rem(gy + COLS - k, COLS)
            send_z(turn, peer, peer).wait_recv()

        for a in range(3):
            for q in range(3):
                value = in_y[turn, :, q * 3 + a]
                for bit in range(4):
                    value = exchange_bit(value, 1 << bit, 3 + bit)
                high, low = split(value.reshape(128, 128))
                rows_y[pl.ds(a * 128, 128), pl.ds(q * 128, 128)] = high
                rows_y[pl.ds(a * 128, 128), pl.ds(N + q * 128, 128)] = high
                rows_y[pl.ds(a * 128, 128), pl.ds(2 * N + q * 128, 128)] = low
        product = lax.dot_general(second[...], rows_y[...], NT, preferred_element_type=F32)
        for a in range(3):
            part = combine(product[:, a * 128 : a * 128 + 128])
            out_y[turn, :, a] = part.reshape(ROWS, 24, 128)
        own_y(turn).start()

        @pl.loop(1, ROWS)
        def _(k):
            send_y(turn, lax.rem(gx + k, ROWS), gx).start()

    for turn in range(ROUNDS):
        own_y(turn).wait()

        @pl.loop(1, ROWS)
        def _(k):
            peer = lax.rem(gx + ROWS - k, ROWS)
            send_y(turn, peer, peer).wait_recv()

        value = in_x[turn].reshape(ROWS, 72, 128)
        value = exchange_bit(value, 4, 6)
        value = exchange_bit(value, 2, 1)
        value = exchange_bit(value, 1, 0)
        high, low = split(value.reshape(576, 128))
        rows_x[:, pl.ds(turn * 128, 128)] = high
        rows_x[:, pl.ds(N + turn * 128, 128)] = high
        rows_x[:, pl.ds(2 * N + turn * 128, 128)] = low

    cos = jnp.dot(rows_x[...], first_cos[...], preferred_element_type=F32)
    sin = jnp.dot(rows_x[...], first_sin[...], preferred_element_type=F32)
    real = (cos[:288] - sin[288:]).reshape(4, 3, 24, M)
    imag = (sin[:288] + cos[288:]).reshape(4, 3, 24, M)
    for b in range(4):
        for a in range(3):
            out[0, a * 4 + b] = real[b, a]
            out[1, a * 4 + b] = imag[b, a]

    for turn in range(ROUNDS):

        @pl.loop(1, COLS)
        def _(k):
            send_z(turn, lax.rem(gy + k, COLS), gy).wait_send()

        @pl.loop(1, ROWS)
        def _(k):
            send_y(turn, lax.rem(gx + k, ROWS), gx).wait_send()


def transform(grid, third, second, first_cos, first_sin):
    vmem = pl.BlockSpec(memory_space=pltpu.VMEM)
    return pl.pallas_call(
        transform_kernel,
        out_shape=jax.ShapeDtypeStruct((2, 12, 24, M), F32),
        in_specs=[vmem] * 5,
        out_specs=vmem,
        scratch_shapes=[
            pltpu.VMEM((ROUNDS, 8, 2, 9, 8, 128), F32),
            pltpu.VMEM((ROUNDS, COLS, 9, 8, 128), F32),
            pltpu.VMEM((N, 3 * N), BF16),
            pltpu.VMEM((ROUNDS, ROWS, 3, 24, 128), F32),
            pltpu.VMEM((ROUNDS, ROWS, 3, 24, 128), F32),
            pltpu.VMEM((576, 3 * N), BF16),
            pltpu.SemaphoreType.DMA((ROUNDS, COLS)),
            pltpu.SemaphoreType.DMA((ROUNDS, COLS)),
            pltpu.SemaphoreType.DMA((ROUNDS, ROWS)),
            pltpu.SemaphoreType.DMA((ROUNDS, ROWS)),
            pltpu.SemaphoreType.DMA((2, ROUNDS)),
        ],
        compiler_params=pltpu.CompilerParams(has_side_effects=True, vmem_limit_bytes=48 << 20),
        name="transform",
    )(grid, third, second, first_cos, first_sin)


def solution(mesh):
    third, second, first_cos, first_sin = tables()

    def on_device(samples, kernel, offsets, owners, tile_ids, deapod_first, deapod_second, deapod_third):
        outbox = spread(owners[:, 0], tile_ids, samples, kernel, offsets)
        grid = gather(route(outbox))
        along_x = transform(grid, third, second, first_cos, first_sin)
        return (
            along_x
            * deapod_third[None, :, None, None]
            * deapod_second[None, None, :, None]
            * deapod_first[None, None, None, :]
        )

    in_specs = (
        P(("gx", "gy"), None, None),
        P(("gx", "gy"), None, None, None),
        P(("gx", "gy"), None, None),
        P(("gx", "gy"), None),
        P(("gx", "gy")),
        P(),
        P("gx"),
        P("gy"),
    )
    return jax.shard_map(
        on_device, mesh=mesh, in_specs=in_specs, out_specs=P(None, "gy", "gx", None), check_vma=False
    )
```

time: 444 us -> 94.6 us (0.21); the launches traced: 436 us -> 94.4 us
  local copies, waits for them, and re-layouts: 172 us -> 6.2 us
  matrix products: 156 us -> 0 us
  Pallas kernels: 0 us -> 87 us
  blocking collectives: 45.6 us -> 0 us
  waiting for transfers between devices: 31.9 us -> 0 us
  other arithmetic: 17.9 us -> 1.01 us
  starting transfers between devices: 11.5 us -> 0 us
    dot_general x14 -> x0, matrix products: 156 us -> none  [the longest x1 114 us: spread(): jnp.einsum('nijs,ncls->ncijl', plane_weight, depth_weight, precision=lax....]
    pallas_call x0 -> x4, Pallas kernels: none -> 87 us  [the longest x1 42 us: transform(): pl.pallas_call(transform_kernel, out_shape=jax.ShapeDtypeStruct((2, 12, 2...]
    squeeze x6 -> x0, local copies, waits for them, and re-layouts: 75.8 us -> none  [the longest x2 37.7 us: on_device(): spread_grid[0]]
    all_to_all x2 -> x0, blocking collectives: 45.6 us -> none  [the longest x1 27.9 us: on_device(): lax.all_to_all(along_z, 'gy', split_axis=1, concat_axis=3, tiled=True)]
    all_to_all x1 -> x0, waiting for transfers between devices: 31.9 us -> none  [on_device(): lax.all_to_all(outbox, ('gx', 'gy'), split_axis=0, concat_axis=0, tiled=T...]
    slice x12 -> x0, local copies, waits for them, and re-layouts: 15.7 us -> none  [the longest x1 13.8 us: on_device(): spread_grid[1]]
    scatter x2 -> x0, local copies, waits for them, and re-layouts: 15.7 us -> none  [on_device(): outbox = outbox.at[target, position].set(payload)]
    unnamed x16 -> x25, local copies, waits for them, and re-layouts: 21.3 us -> 6.2 us
  transfers between devices with their start and end apart: 1 -> 0, of which waited for: 1 -> 0; matrix products, arithmetic and copies ran while one was open for 0% -> 0% of each run, Pallas kernels for 0% -> 0%
where the time goes in v1:
time: 94.6 us; the launch traced here: 94.4 us
  Pallas kernels  87 us (92%)
  local copies, waits for them, and re-layouts  6.2 us (7%)
  other arithmetic  1.01 us (1%)
    pallas_call x1, Pallas kernels, transform(): pl.pallas_call(transform_kernel, out_shape=jax.ShapeDtypeStruct((2, 12, 2...  42 us
    pallas_call x1, Pallas kernels, route(): pl.pallas_call(route_kernel, out_shape=jax.ShapeDtypeStruct(outbox.shape,...  33.9 us
    pallas_call x1, Pallas kernels, spread(): pl.pallas_call(spread_kernel, out_shape=jax.ShapeDtypeStruct((DEVICES, SL...  9.1 us
    unnamed x25, local copies, waits for them, and re-layouts  6.2 us
    pallas_call x1, Pallas kernels, gather(): pl.pallas_call(gather_kernel, out_shape=jax.ShapeDtypeStruct((TILES + 1,...  1.95 us

profile of v1, /device:TPU:1, one launch (start us, length us, event | category | flops | bytes accessed | tf_op | source)
XLA Modules:
  0.0 94.4 jit_solution(3589644084710222161)
XLA Ops:
  0.0 1.1 %copy.13.offsets = s32[128,3,128]{2,1,0:T(4,128)S(1)} copy(s32[128,3,128]{2,0,1:T(8,128)} %param.14) | data formatting | bytes 393216 | tf_op args[2]
  1.1 0.0 copy-start.3
  1.1 1.1 %copy-done.3 = f32[128,3,4,128]{3,2,1,0:T(4,128)S(1)} copy-done((f32[128,3,4,128]{3,2,1,0:T(4,128)S(1)}, f32[128,3,4,128]{3,2,1,0:T(4,128)}, u32[]{:S(2)}) %copy-start.3) | copy-done | bytes 786456
  2.2 0.0 copy-start.6
  2.2 0.9 copy-done.6
  3.1 0.0 copy-start.7
  3.1 0.7 copy-done.7
  3.8 0.0 copy-start.8
  3.8 0.7 copy-done.8
  4.4 9.1 %spread.1.x = f32[128,17,128]{2,1,0:T(8,128)S(1)} custom-call(s32[128]{0:T(128)S(1)} %bitcast.1, s32[128]{0:T(128)S(1)} %copy-done.8, f32[128,2,128]{2,1,0:T(2,128)S(1)} %copy-done.6, f32[128,3,4,128]{3,2,1,0:T(4,128)S(1)} %copy-done.3, s32[128,3,128]{2,1,0:T(4,128)S(1)} %copy.13.offsets), custom_call_target="tpu_custom_call" | custom-call | tf_op jit(solution)/shard_map/spread/pallas_call | solution.py:146
  13.5 33.9 %route.1.inbox = f32[128,17,128]{2,1,0:T(8,128)S(1)} custom-call(f32[128,17,128]{2,1,0:T(8,128)S(1)} %spread.1.x), custom_call_target="tpu_custom_call" | custom-call | tf_op jit(solution)/shard_map/route/pallas_call | solution.py:191
  47.5 0.0 copy-start.1
  47.5 0.0 copy-start.2
  47.5 0.0 copy-start.4
  47.5 0.0 copy-start.5
  47.5 1.9 %gather.1.grid = f32[865,8,128]{2,1,0:T(8,128)S(1)} custom-call(f32[128,17,128]{2,1,0:T(8,128)S(1)} %route.1.inbox), custom_call_target="tpu_custom_call" | custom-call | tf_op jit(solution)/shard_map/gather/pallas_call | solution.py:230
  49.5 0.0 copy-start
  49.5 1.7 %copy-done = f32[865,8,128]{2,1,0:T(8,128)} copy-done((f32[865,8,128]{2,1,0:T(8,128)}, f32[865,8,128]{2,1,0:T(8,128)S(1)}, u32[]{:S(2)}) %copy-start) | copy-done | bytes 3543064
  51.2 0.0 copy-done.1
  51.2 0.0 copy-done.2
  51.2 0.0 copy-done.4
  51.2 0.0 copy-done.5
  51.3 0.0 copy-start.9
  51.3 0.0 copy-start.10
  51.3 0.0 copy-start.11
  51.3 42.0 %transform.1 = f32[2,12,24,192]{3,2,1,0:T(8,128)S(1)} custom-call(f32[865,8,128]{2,1,0:T(8,128)} %copy-done, bf16[384,1152]{1,0:T(8,128)(2,1)S(1)} %copy-done.2, bf16[384,1152]{1,0:T(8,128)(2,1)S(1)} %copy-done.1, bf16[1152,192]{1,0:T(8,128)(2,1)S(1)} %copy-done.5, bf16[1152,192]{1,0:T(8,128)(2,1)S(1)} %copy-done.4), custom_call_target="tpu_custom_call" | custom-call | tf_op jit(solution)/shard_map/transform/pallas_call | solution.py:387
  93.3 0.0 copy-done.9
  93.3 0.0 copy-done.10
  93.3 0.0 copy-done.11
  93.3 1.0 %multiply_multiply_fusion = f32[2,12,24,192]{3,2,1,0:T(8,128)} fusion(f32[2,12,24,192]{3,2,1,0:T(8,128)S(1)} %transform.1, f32[192]{0:T(256)S(1)} %copy-done.9, f32[24]{0:T(128)S(1)} %copy-done.10, f32[12]{0:T(128)S(1)} %copy-done.11), kind=kLoop, calls=%fused_computation | loop fusion | flops 331776 | bytes 885648 | tf_op jit(solution)/shard_map/mul | solution.py:418
Async XLA Ops:
  1.1 1.1 %copy-start.3 = (f32[128,3,4,128]{3,2,1,0:T(4,128)S(1)}, f32[128,3,4,128]{3,2,1,0:T(4,128)}, u32[]{:S(2)}) copy-start(f32[128,3,4,128]{3,2,1,0:T(4,128)} %kernel.1) | copy-start | bytes 2359300
  2.2 0.9 copy-start.6
  3.1 0.7 copy-start.7
  3.8 0.7 copy-start.8
  47.5 3.8 %copy-start.1 = (bf16[384,1152]{1,0:T(8,128)(2,1)S(1)}, bf16[384,1152]{1,0:T(8,128)(2,1)}, u32[]{:S(2)}) copy-start(bf16[384,1152]{1,0:T(8,128)(2,1)} %constant.9.clone.second) | copy-start | bytes 2654212
  47.5 3.8 %copy-start.2 = (bf16[384,1152]{1,0:T(8,128)(2,1)S(1)}, bf16[384,1152]{1,0:T(8,128)(2,1)}, u32[]{:S(2)}) copy-start(bf16[384,1152]{1,0:T(8,128)(2,1)} %constant.8.clone.third) | copy-start | bytes 2654212
  47.5 3.7 %copy-start.4 = (bf16[1152,192]{1,0:T(8,128)(2,1)S(1)}, bf16[1152,192]{1,0:T(8,128)(2,1)}, u32[]{:S(2)}) copy-start(bf16[1152,192]{1,0:T(8,128)(2,1)} %constant.11.clone.first_sin) | copy-start | bytes 1327108
  47.5 3.7 %copy-start.5 = (bf16[1152,192]{1,0:T(8,128)(2,1)S(1)}, bf16[1152,192]{1,0:T(8,128)(2,1)}, u32[]{:S(2)}) copy-start(bf16[1152,192]{1,0:T(8,128)(2,1)} %constant.10.clone.first_cos) | copy-start | bytes 1327108
  49.5 1.8 %copy-start = (f32[865,8,128]{2,1,0:T(8,128)}, f32[865,8,128]{2,1,0:T(8,128)S(1)}, u32[]{:S(2)}) copy-start(f32[865,8,128]{2,1,0:T(8,128)S(1)} %gather.1.grid) | copy-start | bytes 10629124
  51.3 42.1 %copy-start.9 = (f32[192]{0:T(256)S(1)}, f32[192]{0:T(256)}, u32[]{:S(2)}) copy-start(f32[192]{0:T(256)} %param.17) | copy-start | bytes 2308
  51.3 42.1 %copy-start.10 = (f32[24]{0:T(128)S(1)}, f32[24]{0:T(128)}, u32[]{:S(2)}) copy-start(f32[24]{0:T(128)} %param.18) | copy-start | bytes 292
  51.3 42.1 %copy-start.11 = (f32[12]{0:T(128)S(1)}, f32[12]{0:T(128)}, u32[]{:S(2)}) copy-start(f32[12]{0:T(128)} %param.19) | copy-start | bytes 148

commit v2 on v1

v2 whole, which is shorter than its diff:
```python
import math

import jax
import jax.numpy as jnp
import ml_dtypes
import numpy as np
from jax import lax
from jax.experimental import pallas as pl
from jax.experimental.pallas import tpu as pltpu
from jax.sharding import PartitionSpec as P

N = 384
M = 192
DEVICES = 128
ROWS, COLS = 8, 16
BLOCKS = 128
TILES = 864
SLOT_ROWS = 17
ROUNDS = 3
MESH = pl.DeviceIdType.MESH
F32 = jnp.float32
BF16 = jnp.bfloat16


def angles(cells, images):
    steps = np.mod((cells[:, None] - N // 2) * (images[None, :] - M // 2), N)
    phases = steps.astype(np.float64) * (2.0 * math.pi / N)
    return np.cos(phases) / math.sqrt(N), np.sin(phases) / math.sqrt(N)


def halves(table):
    table = table.astype(np.float32)
    high = table.astype(ml_dtypes.bfloat16)
    low = (table - high.astype(np.float32)).astype(ml_dtypes.bfloat16)
    return high, low


def left_table(cells, images):
    cos, sin = angles(cells, images)
    high, low = halves(np.concatenate((cos.T, sin.T)))
    return np.concatenate((high, low, high), axis=1)


def tables():
    every = np.arange(M)
    a, pair, side, low = np.meshgrid(np.arange(3), np.arange(8), np.arange(2), np.arange(4), indexing="ij")
    order = (12 * (2 * pair + side) + 4 * a + low).reshape(-1)
    l, d = np.meshgrid(np.arange(8), np.arange(48), indexing="ij")
    third = left_table((d * 8 + l).reshape(-1), order)
    q, g, j = np.meshgrid(np.arange(3), np.arange(COLS), np.arange(8), indexing="ij")
    second = left_table((g * 24 + q * 8 + j).reshape(-1), every)
    turn, lane = np.meshgrid(np.arange(ROUNDS), np.arange(128), indexing="ij")
    source = (lane >> 6) * 4 + (lane & 3)
    cells = source * 48 + (2 * turn + ((lane >> 2) & 1)) * 8 + ((lane >> 3) & 7)
    firsts = []
    for part in angles(cells.reshape(-1), every):
        high, low = halves(part)
        firsts.append(np.concatenate((high, low, high), axis=0))
    return third, second, firsts[0], firsts[1]


def split(value):
    high = value.astype(BF16)
    return high, (value - high.astype(F32)).astype(BF16)


def exchange_bit(value, axis_low, lane_bit):
    count, rows, lanes = value.shape
    shift = 1 << lane_bit
    pairs = value.reshape(count // (2 * axis_low), 2, axis_low * rows, lanes)
    first = pairs[:, 0].reshape(-1, lanes)
    second = pairs[:, 1].reshape(-1, lanes)
    lane = lax.broadcasted_iota(jnp.int32, first.shape, 1)
    upper = (lane & shift) != 0
    new_first = jnp.where(upper, pltpu.roll(second, shift, 1), first)
    new_second = jnp.where(upper, second, pltpu.roll(first, lanes - shift, 1))
    shape = (count // (2 * axis_low), axis_low * rows, lanes)
    out = jnp.stack((new_first.reshape(shape), new_second.reshape(shape)), axis=1)
    return out.reshape(value.shape)


def combine(product):
    rows = product.shape[0] // 2
    lane = lax.broadcasted_iota(jnp.int32, (rows, 128), 1)
    turned = pltpu.roll(product[rows:], 64, 1)
    return product[:rows] + jnp.where(lane < 64, -turned, turned)


NT = (((1,), (1,)), ((), ()))


def whole_kernel(
    owners_in,
    tile_ids_in,
    samples_in,
    kernel_in,
    offsets_in,
    third_in,
    second_in,
    first_cos_in,
    first_sin_in,
    out,
    owners,
    tile_ids,
    samples,
    kernel,
    offsets,
    third,
    second,
    first_cos,
    first_sin,
    pieces,
    ids,
    source_of,
    slots,
    outbox,
    inbox,
    marks,
    arrived,
    cells,
    out_z,
    in_y,
    rows_y,
    out_y,
    in_x,
    rows_x,
    load_sem,
    slot_sem,
    p_send,
    p_recv,
    z_send,
    z_recv,
    y_send,
    y_recv,
    own_sem,
):
    gx, gy = lax.axis_index("gx"), lax.axis_index("gy")
    me = gx * COLS + gy

    loads = [
        pltpu.make_async_copy(source, target, load_sem.at[i])
        for i, (source, target) in enumerate(
            (
                (owners_in, owners),
                (tile_ids_in, tile_ids),
                (offsets_in, offsets),
                (samples_in, samples),
                (kernel_in, kernel),
                (third_in, third),
                (second_in, second),
                (first_cos_in, first_cos),
                (first_sin_in, first_sin),
            )
        )
    ]
    for load in loads:
        load.start()
    barrier = pltpu.get_barrier_semaphore()

    def greet(k):
        peer = lax.rem(me + k, DEVICES)
        pl.semaphore_signal(
            barrier, inc=1, device_id=(peer // COLS, lax.rem(peer, COLS)), device_id_type=MESH
        )

    loads[0].wait()
    loads[1].wait()
    lane = lax.broadcasted_iota(jnp.int32, (128, 128), 1)
    block = lax.broadcasted_iota(jnp.int32, (128, 128), 0)
    named = jnp.transpose(jnp.broadcast_to(owners[...], (128, 128))) == lane
    tiles = jnp.transpose(jnp.broadcast_to(tile_ids[...], (128, 128)))
    first = jnp.min(jnp.where(named, block, BLOCKS), axis=0, keepdims=True)
    last = jnp.max(jnp.where(named, block, -1), axis=0, keepdims=True)
    last = jnp.where(last > first, last, BLOCKS)
    source_of[pl.ds(0, 1), :] = first
    source_of[pl.ds(1, 1), :] = last
    place_slots = pltpu.make_async_copy(source_of, slots, slot_sem)
    place_slots.start()
    found = []
    for chosen in (first, last):
        tile = jnp.sum(jnp.where(named & (block == chosen), tiles, 0), axis=0, keepdims=True)
        found.append(jnp.where(chosen < BLOCKS, tile, TILES).astype(F32))
    low_lane = lax.broadcasted_iota(jnp.int32, (1, 128), 1) < 64
    ids[pl.ds(0, 1), :] = jnp.where(low_lane, found[0], pltpu.roll(found[1], 64, 1))
    ids[pl.ds(1, 1), :] = jnp.where(low_lane, pltpu.roll(found[0], 64, 1), found[1])

    for load in loads[2:5]:
        load.wait()
    pieces[BLOCKS] = jnp.zeros((8, 128), F32)
    cell = lax.broadcasted_iota(jnp.int32, (8, 128), 0)

    @pl.loop(0, BLOCKS // 8)
    def _(step):
        starts = [offsets[dim, pl.ds(pl.multiple_of(step * 8, 8), 8), :] for dim in range(3)]
        for u in range(8):
            n = step * 8 + u

            @pl.when(n > 0)
            def _():
                greet(n)

            placed = []
            for dim in range(3):
                away = cell - starts[dim][u : u + 1]
                total = jnp.zeros((8, 128), F32)
                for k in range(4):
                    total = jnp.where(away == k, kernel[n, dim, pl.ds(k, 1), :], total)
                placed.append(total)
            real = samples[n, pl.ds(0, 1), :] * placed[0]
            imag = samples[n, pl.ds(1, 1), :] * placed[0]
            plane = jnp.concatenate((real, imag), axis=0)
            weight = (plane[:, None, :] * placed[1][None, :, :]).reshape(128, 128)
            high, low = split(weight)
            depth_high, depth_low = split(placed[2])
            left = jnp.concatenate(
                (
                    jnp.concatenate((depth_high, depth_high), axis=1),
                    jnp.concatenate((depth_low, jnp.zeros_like(depth_low)), axis=1),
                ),
                axis=0,
            )
            right = jnp.concatenate((high, low), axis=1)
            both = lax.dot_general(left, right, NT, preferred_element_type=F32)
            pieces[n] = both[:8] + both[8:]

    place_slots.wait()
    pl.semaphore_wait(barrier, DEVICES - 1)

    def send_piece(peer, lands):
        return pltpu.make_async_remote_copy(
            src_ref=outbox.at[peer],
            dst_ref=inbox.at[lands],
            send_sem=p_send.at[peer],
            recv_sem=p_recv.at[lands],
            device_id=(peer // COLS, lax.rem(peer, COLS)),
            device_id_type=MESH,
        )

    def fill(box, place, peer):
        box[place, pl.ds(0, 8), :] = pieces[slots[0, peer]]
        box[place, pl.ds(8, 8), :] = pieces[slots[1, peer]]
        box[place, pl.ds(16, 1), :] = ids[pl.ds(peer // 64, 1), :]

    @pl.loop(1, DEVICES)
    def _(k):
        peer = lax.rem(me + k, DEVICES)
        fill(outbox, peer, peer)
        send_piece(peer, me).start()

    fill(inbox, me, me)

    @pl.loop(0, ROWS)
    def _(t):
        group = lax.rem(gx + ROWS - t, ROWS)

        @pl.loop(0, COLS)
        def _(u):
            peer = group * COLS + u

            @pl.when(peer != me)
            def _():
                send_piece(peer, peer).wait_recv()

        base = pl.multiple_of(group * COLS, COLS)
        for slot in range(2):
            for l in range(8):
                high, low = split(inbox[pl.ds(base, COLS), slot * 8 + l, :])
                arrived[pl.ds(pl.multiple_of(base + slot * 128, 16), COLS), pl.ds(l * 128, 128)] = high
                arrived[pl.ds(pl.multiple_of(base + 256 + slot * 128, 16), COLS), pl.ds(l * 128, 128)] = low

    marks[...] = jnp.transpose(inbox[:, 16, :])
    mine = lax.rem(me, 64)
    tile_rows = [marks[pl.ds(mine + 64 * slot, 1), :] for slot in range(2)]
    for load in loads[5:]:
        load.wait()

    def send_z(turn, peer, lands):
        return pltpu.make_async_remote_copy(
            src_ref=out_z.at[turn, peer // 2, lax.rem(peer, 2)],
            dst_ref=in_y.at[turn, lands],
            send_sem=z_send.at[turn, peer],
            recv_sem=z_recv.at[turn, lands],
            device_id=(gx, peer),
            device_id_type=MESH,
        )

    def own_z(turn):
        return pltpu.make_async_copy(
            out_z.at[turn, gy // 2, lax.rem(gy, 2)], in_y.at[turn, gy], own_sem.at[0, turn]
        )

    def send_y(turn, peer, lands):
        return pltpu.make_async_remote_copy(
            src_ref=out_y.at[turn, peer],
            dst_ref=in_x.at[turn, lands],
            send_sem=y_send.at[turn, peer],
            recv_sem=y_recv.at[turn, lands],
            device_id=(peer, gy),
            device_id_type=MESH,
        )

    def own_y(turn):
        return pltpu.make_async_copy(out_y.at[turn, gx], in_x.at[turn, gx], own_sem.at[1, turn])

    row = lax.broadcasted_iota(jnp.int32, (24, 8, 128), 1)
    share = TILES // ROUNDS
    tile_of = lax.broadcasted_iota(jnp.int32, (share, 128), 0)
    for turn in range(ROUNDS):
        hits = [
            jnp.where((tile_of + turn * share).astype(F32) == tile_row, 1.0, 0.0).astype(BF16)
            for tile_row in tile_rows
        ]
        hits = jnp.concatenate(hits + hits, axis=1)
        for pair in range(4):
            added = jnp.dot(hits, arrived[:, pl.ds(pair * 256, 256)], preferred_element_type=F32)
            for half, value in enumerate(split(added)):
                for l in range(2):
                    for column in range(6):
                        cells[half, column, pl.ds((2 * pair + l) * 48, 48), :] = value[
                            column * 48 : column * 48 + 48, l * 128 : l * 128 + 128
                        ]
        for q in range(3):
            high, low = [
                jnp.concatenate((cells[half, q], cells[half, 3 + q]), axis=1) for half in range(2)
            ]
            product = jnp.dot(
                third[...], jnp.concatenate((high, high, low), axis=0), preferred_element_type=F32
            )
            near = combine(product[:, :128]).reshape(24, 8, 128)
            far = combine(product[:, 128:]).reshape(24, 8, 128)
            even = jnp.where(row < 4, near, pltpu.roll(far, 4, 1))
            odd = jnp.where(row < 4, pltpu.roll(near, 4, 1), far)
            for a in range(3):
                out_z[turn, :, 0, q * 3 + a] = even[a * 8 : a * 8 + 8]
                out_z[turn, :, 1, q * 3 + a] = odd[a * 8 : a * 8 + 8]
        own_z(turn).start()

        @pl.loop(1, COLS)
        def _(k):
            send_z(turn, lax.rem(gy + k, COLS), gy).start()

    for turn in range(ROUNDS):
        own_z(turn).wait()

        @pl.loop(1, COLS)
        def _(k):
            peer = lax.rem(gy + COLS - k, COLS)
            send_z(turn, peer, peer).wait_recv()

        for a in range(3):
            for q in range(3):
                value = in_y[turn, :, q * 3 + a]
                for bit in range(4):
                    value = exchange_bit(value, 1 << bit, 3 + bit)
                high, low = split(value.reshape(128, 128))
                rows_y[pl.ds(a * 128, 128), pl.ds(q * 128, 128)] = high
                rows_y[pl.ds(a * 128, 128), pl.ds(N + q * 128, 128)] = high
                rows_y[pl.ds(a * 128, 128), pl.ds(2 * N + q * 128, 128)] = low
        product = lax.dot_general(second[...], rows_y[...], NT, preferred_element_type=F32)
        for a in range(3):
            part = combine(product[:, a * 128 : a * 128 + 128])
            out_y[turn, :, a] = part.reshape(ROWS, 24, 128)
        own_y(turn).start()

        @pl.loop(1, ROWS)
        def _(k):
            send_y(turn, lax.rem(gx + k, ROWS), gx).start()

    for turn in range(ROUNDS):
        own_y(turn).wait()

        @pl.loop(1, ROWS)
        def _(k):
            peer = lax.rem(gx + ROWS - k, ROWS)
            send_y(turn, peer, peer).wait_recv()

        value = in_x[turn].reshape(ROWS, 72, 128)
        value = exchange_bit(value, 4, 6)
        value = exchange_bit(value, 2, 1)
        value = exchange_bit(value, 1, 0)
        high, low = split(value.reshape(576, 128))
        rows_x[:, pl.ds(turn * 128, 128)] = high
        rows_x[:, pl.ds(N + turn * 128, 128)] = high
        rows_x[:, pl.ds(2 * N + turn * 128, 128)] = low

    cos = jnp.dot(rows_x[...], first_cos[...], preferred_element_type=F32)
    sin = jnp.dot(rows_x[...], first_sin[...], preferred_element_type=F32)
    real = (cos[:288] - sin[288:]).reshape(4, 3, 24, M)
    imag = (sin[:288] + cos[288:]).reshape(4, 3, 24, M)
    for b in range(4):
        for a in range(3):
            out[0, a * 4 + b] = real[b, a]
            out[1, a * 4 + b] = imag[b, a]

    for turn in range(ROUNDS):

        @pl.loop(1, COLS)
        def _(k):
            send_z(turn, lax.rem(gy + k, COLS), gy).wait_send()

        @pl.loop(1, ROWS)
        def _(k):
            send_y(turn, lax.rem(gx + k, ROWS), gx).wait_send()


    @pl.loop(1, DEVICES)
    def _(k):
        send_piece(lax.rem(me + k, DEVICES), me).wait_send()


def whole(owners, tile_ids, samples, kernel, offsets, third, second, first_cos, first_sin):
    operands = (owners, tile_ids, samples, kernel, offsets, third, second, first_cos, first_sin)
    held = [pltpu.VMEM(x.shape, x.dtype) for x in operands]
    return pl.pallas_call(
        whole_kernel,
        out_shape=jax.ShapeDtypeStruct((2, 12, 24, M), F32),
        in_specs=[pl.BlockSpec(memory_space=pl.ANY)] * len(operands),
        out_specs=pl.BlockSpec(memory_space=pltpu.VMEM),
        scratch_shapes=held
        + [
            pltpu.VMEM((BLOCKS + 1, 8, 128), F32),
            pltpu.VMEM((8, 128), F32),
            pltpu.VMEM((8, 128), jnp.int32),
            pltpu.SMEM((8, 128), jnp.int32),
            pltpu.VMEM((DEVICES, SLOT_ROWS, 128), F32),
            pltpu.VMEM((DEVICES, SLOT_ROWS, 128), F32),
            pltpu.VMEM((128, 128), F32),
            pltpu.VMEM((512, 1024), BF16),
            pltpu.VMEM((2, 6, N, 128), BF16),
            pltpu.VMEM((ROUNDS, 8, 2, 9, 8, 128), F32),
            pltpu.VMEM((ROUNDS, COLS, 9, 8, 128), F32),
            pltpu.VMEM((N, 3 * N), BF16),
            pltpu.VMEM((ROUNDS, ROWS, 3, 24, 128), F32),
            pltpu.VMEM((ROUNDS, ROWS, 3, 24, 128), F32),
            pltpu.VMEM((576, 3 * N), BF16),
            pltpu.SemaphoreType.DMA((len(operands),)),
            pltpu.SemaphoreType.DMA,
            pltpu.SemaphoreType.DMA((DEVICES,)),
            pltpu.SemaphoreType.DMA((DEVICES,)),
            pltpu.SemaphoreType.DMA((ROUNDS, COLS)),
            pltpu.SemaphoreType.DMA((ROUNDS, COLS)),
            pltpu.SemaphoreType.DMA((ROUNDS, ROWS)),
            pltpu.SemaphoreType.DMA((ROUNDS, ROWS)),
            pltpu.SemaphoreType.DMA((2, ROUNDS)),
        ],
        compiler_params=pltpu.CompilerParams(
            collective_id=0, has_side_effects=True, vmem_limit_bytes=48 << 20
        ),
        name="whole",
    )(*operands)


def solution(mesh):
    third, second, first_cos, first_sin = tables()

    def on_device(samples, kernel, offsets, owners, tile_ids, deapod_first, deapod_second, deapod_third):
        along_x = whole(
            owners.reshape(1, BLOCKS),
            tile_ids.reshape(1, BLOCKS),
            samples,
            kernel,
            offsets.transpose(1, 0, 2),
            third,
            second,
            first_cos,
            first_sin,
        )
        return (
            along_x
            * deapod_third[None, :, None, None]
            * deapod_second[None, None, :, None]
            * deapod_first[None, None, None, :]
        )

    in_specs = (
        P(("gx", "gy"), None, None),
        P(("gx", "gy"), None, None, None),
        P(("gx", "gy"), None, None),
        P(("gx", "gy"), None),
        P(("gx", "gy")),
        P(),
        P("gx"),
        P("gy"),
    )
    return jax.shard_map(
        on_device, mesh=mesh, in_specs=in_specs, out_specs=P(None, "gy", "gx", None), check_vma=False
    )
```

time: 94.6 us -> 95.2 us (level)
  Pallas kernels: 87 us -> 85 us
  local copies, waits for them, and re-layouts: 6.2 us -> 8.1 us
    pallas_call x4 -> x1, Pallas kernels: 87 us -> 85 us  [whole(): pl.pallas_call(whole_kernel, out_shape=jax.ShapeDtypeStruct((2, 12, 24, M...]
    unnamed x25 -> x24, local copies, waits for them, and re-layouts: 6.2 us -> 8.1 us
where the time goes in v2:
time: 95.2 us; the launch traced here: 94.2 us
  Pallas kernels  85 us (89%)
  local copies, waits for them, and re-layouts  8.1 us (9%)
  other arithmetic  1.01 us (1%)
    pallas_call x1, Pallas kernels, whole(): pl.pallas_call(whole_kernel, out_shape=jax.ShapeDtypeStruct((2, 12, 24, M...  85 us
    unnamed x24, local copies, waits for them, and re-layouts  8.1 us

profile of v2, /device:TPU:1, one launch (start us, length us, event | category | flops | bytes accessed | tf_op | source)
XLA Modules:
  0.0 94.2 jit_solution(13696332133152738563)
XLA Ops:
  0.0 0.0 copy-start.7
  0.0 0.0 copy-start.8
  0.0 0.7 copy-done.7
  0.7 0.0 copy-done.8
  0.7 0.0 copy-start
  0.7 1.2 %copy-done = bf16[384,1152]{1,0:T(8,128)(2,1)S(1)} copy-done((bf16[384,1152]{1,0:T(8,128)(2,1)S(1)}, bf16[384,1152]{1,0:T(8,128)(2,1)}, u32[]{:S(2)}) %copy-start) | copy-done | bytes 884760
  1.8 0.0 copy-start.1
  1.8 1.2 %copy-done.1 = bf16[384,1152]{1,0:T(8,128)(2,1)S(1)} copy-done((bf16[384,1152]{1,0:T(8,128)(2,1)S(1)}, bf16[384,1152]{1,0:T(8,128)(2,1)}, u32[]{:S(2)}) %copy-start.1) | copy-done | bytes 884760
  3.0 0.0 copy-start.2
  3.0 1.1 %copy-done.2 = f32[128,3,4,128]{3,2,1,0:T(4,128)S(1)} copy-done((f32[128,3,4,128]{3,2,1,0:T(4,128)S(1)}, f32[128,3,4,128]{3,2,1,0:T(4,128)}, u32[]{:S(2)}) %copy-start.2) | copy-done | bytes 786456
  4.1 0.0 copy-start.3
  4.1 1.1 %copy-done.3 = bf16[1152,192]{1,0:T(8,128)(2,1)S(1)} copy-done((bf16[1152,192]{1,0:T(8,128)(2,1)S(1)}, bf16[1152,192]{1,0:T(8,128)(2,1)}, u32[]{:S(2)}) %copy-start.3) | copy-done | bytes 442392
  5.2 0.0 copy-start.4
  5.2 1.1 %copy-done.4 = bf16[1152,192]{1,0:T(8,128)(2,1)S(1)} copy-done((bf16[1152,192]{1,0:T(8,128)(2,1)S(1)}, bf16[1152,192]{1,0:T(8,128)(2,1)}, u32[]{:S(2)}) %copy-start.4) | copy-done | bytes 442392
  6.3 0.0 copy-start.5
  6.3 0.9 copy-done.5
  7.2 0.0 copy-start.6
  7.2 0.9 copy-done.6
  8.1 0.0 copy-start.9
  8.1 0.0 copy-start.10
  8.1 0.0 copy-start.11
  8.1 85.0 %whole.1 = f32[2,12,24,192]{3,2,1,0:T(8,128)S(1)} custom-call(s32[1,128]{1,0:T(1,128)S(1)} %bitcast.4, s32[1,128]{1,0:T(1,128)S(1)} %bitcast.5, f32[128,2,128]{2,1,0:T(2,128)S(1)} %copy-done.6, f32[128,3,4,128]{3,2,1,0:T(4,128)S(1)} %copy-done.2, s32[3,128,128]{2,1,0:T(8,128)S(1)} %bitcast.3, bf16[384,1152]{1,0:T(8,128)(2,1)S(1)} %copy-done.1, ...), custom_call_target="tpu_custom_call" | custom-call | tf_op jit(solution)/shard_map/whole/pallas_call | solution.py:414
  93.2 0.0 copy-done.9
  93.2 0.0 copy-done.10
  93.2 0.0 copy-done.11
  93.2 1.0 %multiply_multiply_fusion = f32[2,12,24,192]{3,2,1,0:T(8,128)} fusion(f32[2,12,24,192]{3,2,1,0:T(8,128)S(1)} %whole.1, f32[192]{0:T(256)S(1)} %copy-done.9, f32[24]{0:T(128)S(1)} %copy-done.10, f32[12]{0:T(128)S(1)} %copy-done.11), kind=kLoop, calls=%fused_computation | loop fusion | flops 331776 | bytes 885648 | tf_op jit(solution)/shard_map/mul | solution.py:469
Async XLA Ops:
  0.0 0.7 copy-start.7
  0.0 0.7 copy-start.8
  0.7 1.2 %copy-start = (bf16[384,1152]{1,0:T(8,128)(2,1)S(1)}, bf16[384,1152]{1,0:T(8,128)(2,1)}, u32[]{:S(2)}) copy-start(bf16[384,1152]{1,0:T(8,128)(2,1)} %constant.9.clone.second_in) | copy-start | bytes 2654212
  1.8 1.2 %copy-start.1 = (bf16[384,1152]{1,0:T(8,128)(2,1)S(1)}, bf16[384,1152]{1,0:T(8,128)(2,1)}, u32[]{:S(2)}) copy-start(bf16[384,1152]{1,0:T(8,128)(2,1)} %constant.8.clone.third_in) | copy-start | bytes 2654212
  3.0 1.1 %copy-start.2 = (f32[128,3,4,128]{3,2,1,0:T(4,128)S(1)}, f32[128,3,4,128]{3,2,1,0:T(4,128)}, u32[]{:S(2)}) copy-start(f32[128,3,4,128]{3,2,1,0:T(4,128)} %kernel_in.1) | copy-start | bytes 2359300
  4.1 1.1 %copy-start.3 = (bf16[1152,192]{1,0:T(8,128)(2,1)S(1)}, bf16[1152,192]{1,0:T(8,128)(2,1)}, u32[]{:S(2)}) copy-start(bf16[1152,192]{1,0:T(8,128)(2,1)} %constant.11.clone.first_sin_in) | copy-start | bytes 1327108
  5.2 1.1 %copy-start.4 = (bf16[1152,192]{1,0:T(8,128)(2,1)S(1)}, bf16[1152,192]{1,0:T(8,128)(2,1)}, u32[]{:S(2)}) copy-start(bf16[1152,192]{1,0:T(8,128)(2,1)} %constant.10.clone.first_cos_in) | copy-start | bytes 1327108
  6.3 0.9 copy-start.5
  7.2 0.9 copy-start.6
  8.1 85.1 %copy-start.9 = (f32[192]{0:T(256)S(1)}, f32[192]{0:T(256)}, u32[]{:S(2)}) copy-start(f32[192]{0:T(256)} %param.17) | copy-start | bytes 2308
  8.1 85.1 %copy-start.10 = (f32[24]{0:T(128)S(1)}, f32[24]{0:T(128)}, u32[]{:S(2)}) copy-start(f32[24]{0:T(128)} %param.18) | copy-start | bytes 292
  8.1 85.1 %copy-start.11 = (f32[12]{0:T(128)S(1)}, f32[12]{0:T(128)}, u32[]{:S(2)}) copy-start(f32[12]{0:T(128)} %param.19) | copy-start | bytes 148

commit v3 on v2

--- a/solution.py
+++ b/solution.py
@@ -157,7 +157,8 @@
         load.start()
     barrier = pltpu.get_barrier_semaphore()
 
-    def greet(k):
+    @pl.loop(1, DEVICES)
+    def _(k):
         peer = lax.rem(me + k, DEVICES)
         pl.semaphore_signal(
             barrier, inc=1, device_id=(peer // COLS, lax.rem(peer, COLS)), device_id_type=MESH
@@ -194,10 +195,6 @@
         starts = [offsets[dim, pl.ds(pl.multiple_of(step * 8, 8), 8), :] for dim in range(3)]
         for u in range(8):
             n = step * 8 + u
-
-            @pl.when(n > 0)
-            def _():
-                greet(n)
 
             placed = []
             for dim in range(3):
@@ -444,7 +441,7 @@
             pltpu.SemaphoreType.DMA((2, ROUNDS)),
         ],
         compiler_params=pltpu.CompilerParams(
-            collective_id=0, has_side_effects=True, vmem_limit_bytes=48 << 20
+            collective_id=0, has_side_effects=True, vmem_limit_bytes=62 << 20
         ),
         name="whole",
     )(*operands)

time: 95.2 us -> 71.8 us (0.75)
  Pallas kernels: 85 us -> 69.5 us
  local copies, waits for them, and re-layouts: 8.1 us -> 0.01 us
  other arithmetic: 1.01 us -> 2.08 us
    pallas_call x1, Pallas kernels: 85 us -> 69.5 us  [whole(): pl.pallas_call(whole_kernel, out_shape=jax.ShapeDtypeStruct((2, 12, 24, M...]
    unnamed x24 -> x6, local copies, waits for them, and re-layouts: 8.1 us -> 0.01 us
    mul x1, other arithmetic: 1.01 us -> 2.08 us  [on_device(): along_x * deapod_third[None, :, None, None]]
where the time goes in v3:
time: 71.8 us; the launch traced here: 71.7 us
  Pallas kernels  69.5 us (97%)
  other arithmetic  2.08 us (3%)
    pallas_call x1, Pallas kernels, whole(): pl.pallas_call(whole_kernel, out_shape=jax.ShapeDtypeStruct((2, 12, 24, M...  69.5 us
    mul x1, other arithmetic, on_device(): along_x * deapod_third[None, :, None, None]  2.08 us

profile of v3, /device:TPU:1, one launch (start us, length us, event | category | flops | bytes accessed | tf_op | source)
XLA Modules:
  0.0 71.7 jit_solution(8019473508373477478)
XLA Ops:
  0.0 0.0 copy-start
  0.0 0.0 copy-start.1
  0.0 0.0 copy-start.2
  0.0 69.5 %whole.1 = f32[2,12,24,192]{3,2,1,0:T(8,128)} custom-call(s32[1,128]{1,0:T(1,128)} %bitcast.4, s32[1,128]{1,0:T(1,128)} %bitcast.5, f32[128,2,128]{2,1,0:T(2,128)} %samples_in.1, f32[128,3,4,128]{3,2,1,0:T(4,128)} %kernel_in.1, s32[3,128,128]{2,1,0:T(8,128)} %bitcast.3, bf16[384,1152]{1,0:T(8,128)(2,1)} %constant.8.clone.third_in, ...), custom_call_target="tpu_custom_call" | custom-call | tf_op jit(solution)/shard_map/whole/pallas_call | solution.py:411
  69.5 0.0 copy-done
  69.6 0.0 copy-done.1
  69.6 0.0 copy-done.2
  69.6 2.1 %multiply_multiply_fusion = f32[2,12,24,192]{3,2,1,0:T(8,128)} fusion(f32[2,12,24,192]{3,2,1,0:T(8,128)} %whole.1, f32[192]{0:T(256)S(1)} %copy-done, f32[24]{0:T(128)S(1)} %copy-done.1, f32[12]{0:T(128)S(1)} %copy-done.2), kind=kLoop, calls=%fused_computation | loop fusion | flops 331776 | bytes 885648 | tf_op jit(solution)/shard_map/mul | solution.py:466
Async XLA Ops:
  0.0 69.6 %copy-start = (f32[192]{0:T(256)S(1)}, f32[192]{0:T(256)}, u32[]{:S(2)}) copy-start(f32[192]{0:T(256)} %param.17) | copy-start | bytes 2308
  0.0 69.6 %copy-start.1 = (f32[24]{0:T(128)S(1)}, f32[24]{0:T(128)}, u32[]{:S(2)}) copy-start(f32[24]{0:T(128)} %param.18) | copy-start | bytes 292
  0.0 69.6 %copy-start.2 = (f32[12]{0:T(128)S(1)}, f32[12]{0:T(128)}, u32[]{:S(2)}) copy-start(f32[12]{0:T(128)} %param.19) | copy-start | bytes 148

commit v4 on v3

--- a/solution.py
+++ b/solution.py
@@ -37,8 +37,7 @@
 
 def left_table(cells, images):
     cos, sin = angles(cells, images)
-    high, low = halves(np.concatenate((cos.T, sin.T)))
-    return np.concatenate((high, low, high), axis=1)
+    return np.concatenate(halves(np.concatenate((cos.T, sin.T))), axis=1)
 
 
 def tables():
@@ -54,8 +53,8 @@
     cells = source * 48 + (2 * turn + ((lane >> 2) & 1)) * 8 + ((lane >> 3) & 7)
     firsts = []
     for part in angles(cells.reshape(-1), every):
-        high, low = halves(part)
-        firsts.append(np.concatenate((high, low, high), axis=0))
+        high, low = halves(part.reshape(ROUNDS, 128, M))
+        firsts.append(np.concatenate((high, low), axis=1))
     return third, second, firsts[0], firsts[1]
 
 
@@ -123,7 +122,9 @@
     rows_y,
     out_y,
     in_x,
-    rows_x,
+    sum_cos,
+    sum_sin,
+    settled,
     load_sem,
     slot_sem,
     p_send,
@@ -132,7 +133,6 @@
     z_recv,
     y_send,
     y_recv,
-    own_sem,
 ):
     gx, gy = lax.axis_index("gx"), lax.axis_index("gy")
     me = gx * COLS + gy
@@ -146,23 +146,34 @@
                 (offsets_in, offsets),
                 (samples_in, samples),
                 (kernel_in, kernel),
-                (third_in, third),
-                (second_in, second),
-                (first_cos_in, first_cos),
-                (first_sin_in, first_sin),
+                (third_in, third.at[:, pl.ds(0, 2 * N)]),
+                (third_in.at[:, pl.ds(0, N)], third.at[:, pl.ds(2 * N, N)]),
+                (second_in, second.at[:, pl.ds(0, 2 * N)]),
+                (second_in.at[:, pl.ds(0, N)], second.at[:, pl.ds(2 * N, N)]),
+                (first_cos_in, first_cos.at[:, pl.ds(0, 256)]),
+                (first_cos_in.at[:, pl.ds(0, 128)], first_cos.at[:, pl.ds(256, 128)]),
+                (first_sin_in, first_sin.at[:, pl.ds(0, 256)]),
+                (first_sin_in.at[:, pl.ds(0, 128)], first_sin.at[:, pl.ds(256, 128)]),
             )
         )
     ]
-    for load in loads:
+    for load in loads[:5]:
         load.start()
     barrier = pltpu.get_barrier_semaphore()
 
-    @pl.loop(1, DEVICES)
+    def greet(semaphore, x, y):
+        pl.semaphore_signal(semaphore, inc=1, device_id=(x, y), device_id_type=MESH)
+
+    @pl.loop(1, COLS)
     def _(k):
-        peer = lax.rem(me + k, DEVICES)
-        pl.semaphore_signal(
-            barrier, inc=1, device_id=(peer // COLS, lax.rem(peer, COLS)), device_id_type=MESH
-        )
+        greet(barrier, gx, lax.rem(gy + k, COLS))
+
+    @pl.loop(1, ROWS)
+    def _(k):
+        greet(barrier, lax.rem(gx + k, ROWS), gy)
+
+    for load in loads[5:]:
+        load.start()
 
     loads[0].wait()
     loads[1].wait()
@@ -190,11 +201,10 @@
     pieces[BLOCKS] = jnp.zeros((8, 128), F32)
     cell = lax.broadcasted_iota(jnp.int32, (8, 128), 0)
 
-    @pl.loop(0, BLOCKS // 8)
-    def _(step):
-        starts = [offsets[dim, pl.ds(pl.multiple_of(step * 8, 8), 8), :] for dim in range(3)]
-        for u in range(8):
-            n = step * 8 + u
+    def spread(step):
+        starts = [offsets[dim, pl.ds(pl.multiple_of(step * 16, 16), 16), :] for dim in range(3)]
+        for u in range(16):
+            n = step * 16 + u
 
             placed = []
             for dim in range(3):
@@ -220,45 +230,50 @@
             both = lax.dot_general(left, right, NT, preferred_element_type=F32)
             pieces[n] = both[:8] + both[8:]
 
+    pl.loop(0, BLOCKS // 32)(spread)
+    pl.semaphore_wait(barrier, COLS + ROWS - 2)
+
+    @pl.loop(1, COLS)
+    def _(k):
+        greet(settled, gx, lax.rem(gy + k, COLS))
+
+    pl.loop(BLOCKS // 32, BLOCKS // 16)(spread)
     place_slots.wait()
-    pl.semaphore_wait(barrier, DEVICES - 1)
+    pl.semaphore_wait(settled, COLS - 1)
+
+    def arrival(target, semaphore):
+        pltpu.make_async_copy(target, target, semaphore).wait()
 
     def send_piece(peer, lands):
         return pltpu.make_async_remote_copy(
             src_ref=outbox.at[peer],
             dst_ref=inbox.at[lands],
-            send_sem=p_send.at[peer],
-            recv_sem=p_recv.at[lands],
+            send_sem=p_send,
+            recv_sem=p_recv.at[lands // COLS],
             device_id=(peer // COLS, lax.rem(peer, COLS)),
             device_id_type=MESH,
         )
 
-    def fill(box, place, peer):
-        box[place, pl.ds(0, 8), :] = pieces[slots[0, peer]]
-        box[place, pl.ds(8, 8), :] = pieces[slots[1, peer]]
-        box[place, pl.ds(16, 1), :] = ids[pl.ds(peer // 64, 1), :]
+    def fill(peer):
+        outbox[peer, pl.ds(0, 8), :] = pieces[slots[0, peer]]
+        outbox[peer, pl.ds(8, 8), :] = pieces[slots[1, peer]]
+        outbox[peer, pl.ds(16, 1), :] = ids[pl.ds(peer // 64, 1), :]
 
     @pl.loop(1, DEVICES)
     def _(k):
         peer = lax.rem(me + k, DEVICES)
-        fill(outbox, peer, peer)
+        fill(peer)
         send_piece(peer, me).start()
 
-    fill(inbox, me, me)
+    fill(me)
+    pltpu.make_async_copy(outbox.at[me], inbox.at[me], p_recv.at[gx]).start()
 
     @pl.loop(0, ROWS)
     def _(t):
         group = lax.rem(gx + ROWS - t, ROWS)
 
-        @pl.loop(0, COLS)
-        def _(u):
-            peer = group * COLS + u
-
-            @pl.when(peer != me)
-            def _():
-                send_piece(peer, peer).wait_recv()
-
         base = pl.multiple_of(group * COLS, COLS)
+        arrival(inbox.at[pl.ds(base, COLS)], p_recv.at[group])
         for slot in range(2):
             for l in range(8):
                 high, low = split(inbox[pl.ds(base, COLS), slot * 8 + l, :])
@@ -271,40 +286,66 @@
     for load in loads[5:]:
         load.wait()
 
-    def send_z(turn, peer, lands):
-        return pltpu.make_async_remote_copy(
-            src_ref=out_z.at[turn, peer // 2, lax.rem(peer, 2)],
-            dst_ref=in_y.at[turn, lands],
-            send_sem=z_send.at[turn, peer],
-            recv_sem=z_recv.at[turn, lands],
-            device_id=(gx, peer),
-            device_id_type=MESH,
-        )
-
-    def own_z(turn):
-        return pltpu.make_async_copy(
-            out_z.at[turn, gy // 2, lax.rem(gy, 2)], in_y.at[turn, gy], own_sem.at[0, turn]
-        )
-
-    def send_y(turn, peer, lands):
-        return pltpu.make_async_remote_copy(
-            src_ref=out_y.at[turn, peer],
-            dst_ref=in_x.at[turn, lands],
-            send_sem=y_send.at[turn, peer],
-            recv_sem=y_recv.at[turn, lands],
-            device_id=(peer, gy),
-            device_id_type=MESH,
-        )
-
-    def own_y(turn):
-        return pltpu.make_async_copy(out_y.at[turn, gx], in_x.at[turn, gx], own_sem.at[1, turn])
+    def tile_at(turn, q, a):
+        return q * 3 + a if turn == 0 else a * 3 + q
+
+    def part(turn, third_of):
+        return pl.ds(0, 9) if turn == 1 else pl.ds(3 * third_of, 3)
+
+    def send_z(turn, third_of):
+        tiles_of = part(turn, third_of)
+        count = turn * 3 + third_of
+
+        @pl.loop(1, COLS)
+        def _(k):
+            peer = lax.rem(gy + k, COLS)
+            pltpu.make_async_remote_copy(
+                src_ref=out_z.at[turn, peer // 2, lax.rem(peer, 2), tiles_of],
+                dst_ref=in_y.at[turn, gy, tiles_of],
+                send_sem=z_send,
+                recv_sem=z_recv.at[count],
+                device_id=(gx, peer),
+                device_id_type=MESH,
+            ).start()
+
+        pltpu.make_async_copy(
+            out_z.at[turn, gy // 2, lax.rem(gy, 2), tiles_of], in_y.at[turn, gy, tiles_of], z_recv.at[count]
+        ).start()
+
+    def wait_z(turn, third_of):
+        arrival(in_y.at[turn, :, part(turn, third_of)], z_recv.at[turn * 3 + third_of])
+
+    def send_y(turn, thirds):
+        count = turn * 3 + thirds.start
+
+        @pl.loop(1, ROWS)
+        def _(k):
+            peer = lax.rem(gx + k, ROWS)
+            pltpu.make_async_remote_copy(
+                src_ref=out_y.at[turn, peer, thirds],
+                dst_ref=in_x.at[turn, gx, thirds],
+                send_sem=y_send,
+                recv_sem=y_recv.at[count],
+                device_id=(peer, gy),
+                device_id_type=MESH,
+            ).start()
+
+        pltpu.make_async_copy(
+            out_y.at[turn, gx, thirds], in_x.at[turn, gx, thirds], y_recv.at[count]
+        ).start()
+
+    def wait_y(turn, thirds):
+        arrival(in_x.at[turn, :, thirds], y_recv.at[turn * 3 + thirds.start])
 
     row = lax.broadcasted_iota(jnp.int32, (24, 8, 128), 1)
-    share = TILES // ROUNDS
-    tile_of = lax.broadcasted_iota(jnp.int32, (share, 128), 0)
-    for turn in range(ROUNDS):
+    tile_of = lax.broadcasted_iota(jnp.int32, (48, 128), 0)
+
+    def stage_z(turn, q):
+        bases = [((2 * turn + r) * 3 + q) * 48 for r in range(2)]
         hits = [
-            jnp.where((tile_of + turn * share).astype(F32) == tile_row, 1.0, 0.0).astype(BF16)
+            jnp.concatenate(
+                [jnp.where((tile_of + base).astype(F32) == tile_row, 1.0, 0.0) for base in bases], axis=0
+            ).astype(BF16)
             for tile_row in tile_rows
         ]
         hits = jnp.concatenate(hits + hits, axis=1)
@@ -312,102 +353,108 @@
             added = jnp.dot(hits, arrived[:, pl.ds(pair * 256, 256)], preferred_element_type=F32)
             for half, value in enumerate(split(added)):
                 for l in range(2):
-                    for column in range(6):
-                        cells[half, column, pl.ds((2 * pair + l) * 48, 48), :] = value[
-                            column * 48 : column * 48 + 48, l * 128 : l * 128 + 128
+                    for r in range(2):
+                        cells[half, pl.ds((2 * pair + l) * 48, 48), pl.ds(r * 128, 128)] = value[
+                            r * 48 : r * 48 + 48, l * 128 : l * 128 + 128
                         ]
-        for q in range(3):
-            high, low = [
-                jnp.concatenate((cells[half, q], cells[half, 3 + q]), axis=1) for half in range(2)
-            ]
-            product = jnp.dot(
-                third[...], jnp.concatenate((high, high, low), axis=0), preferred_element_type=F32
-            )
-            near = combine(product[:, :128]).reshape(24, 8, 128)
-            far = combine(product[:, 128:]).reshape(24, 8, 128)
-            even = jnp.where(row < 4, near, pltpu.roll(far, 4, 1))
-            odd = jnp.where(row < 4, pltpu.roll(near, 4, 1), far)
-            for a in range(3):
-                out_z[turn, :, 0, q * 3 + a] = even[a * 8 : a * 8 + 8]
-                out_z[turn, :, 1, q * 3 + a] = odd[a * 8 : a * 8 + 8]
-        own_z(turn).start()
-
-        @pl.loop(1, COLS)
-        def _(k):
-            send_z(turn, lax.rem(gy + k, COLS), gy).start()
-
-    for turn in range(ROUNDS):
-        own_z(turn).wait()
-
-        @pl.loop(1, COLS)
-        def _(k):
-            peer = lax.rem(gy + COLS - k, COLS)
-            send_z(turn, peer, peer).wait_recv()
-
+        high, low = cells[0], cells[1]
+        product = jnp.dot(
+            third[...], jnp.concatenate((high, high, low), axis=0), preferred_element_type=F32
+        )
+        near = combine(product[:, :128]).reshape(24, 8, 128)
+        far = combine(product[:, 128:]).reshape(24, 8, 128)
+        even = jnp.where(row < 4, near, pltpu.roll(far, 4, 1))
+        odd = jnp.where(row < 4, pltpu.roll(near, 4, 1), far)
         for a in range(3):
+            out_z[turn, :, 0, tile_at(turn, q, a)] = even[a * 8 : a * 8 + 8]
+            out_z[turn, :, 1, tile_at(turn, q, a)] = odd[a * 8 : a * 8 + 8]
+
+    def stage_y(turn, thirds):
+        for a in range(thirds.start, thirds.start + thirds.size):
             for q in range(3):
-                value = in_y[turn, :, q * 3 + a]
+                value = in_y[turn, :, tile_at(turn, q, a)]
                 for bit in range(4):
                     value = exchange_bit(value, 1 << bit, 3 + bit)
                 high, low = split(value.reshape(128, 128))
                 rows_y[pl.ds(a * 128, 128), pl.ds(q * 128, 128)] = high
                 rows_y[pl.ds(a * 128, 128), pl.ds(N + q * 128, 128)] = high
                 rows_y[pl.ds(a * 128, 128), pl.ds(2 * N + q * 128, 128)] = low
-        product = lax.dot_general(second[...], rows_y[...], NT, preferred_element_type=F32)
-        for a in range(3):
-            part = combine(product[:, a * 128 : a * 128 + 128])
-            out_y[turn, :, a] = part.reshape(ROWS, 24, 128)
-        own_y(turn).start()
-
-        @pl.loop(1, ROWS)
-        def _(k):
-            send_y(turn, lax.rem(gx + k, ROWS), gx).start()
+        product = lax.dot_general(
+            second[...],
+            rows_y[pl.ds(thirds.start * 128, thirds.size * 128), :],
+            NT,
+            preferred_element_type=F32,
+        )
+        for a in range(thirds.size):
+            done = combine(product[:, a * 128 : a * 128 + 128])
+            out_y[turn, :, thirds.start + a] = done.reshape(ROWS, 24, 128)
+
+    def stage_x(turn, thirds):
+        values = []
+        for a in range(thirds.start, thirds.start + thirds.size):
+            value = in_x[turn, :, a]
+            value = exchange_bit(value, 4, 6)
+            value = exchange_bit(value, 2, 1)
+            values.append(exchange_bit(value, 1, 0).reshape(192, 128))
+        high, low = split(jnp.concatenate(values, axis=0))
+        rows = jnp.concatenate((high, high, low), axis=1)
+        return [
+            jnp.dot(rows, table[turn], preferred_element_type=F32) for table in (first_cos, first_sin)
+        ]
 
     for turn in range(ROUNDS):
-        own_y(turn).wait()
-
-        @pl.loop(1, ROWS)
-        def _(k):
-            peer = lax.rem(gx + ROWS - k, ROWS)
-            send_y(turn, peer, peer).wait_recv()
-
-        value = in_x[turn].reshape(ROWS, 72, 128)
-        value = exchange_bit(value, 4, 6)
-        value = exchange_bit(value, 2, 1)
-        value = exchange_bit(value, 1, 0)
-        high, low = split(value.reshape(576, 128))
-        rows_x[:, pl.ds(turn * 128, 128)] = high
-        rows_x[:, pl.ds(N + turn * 128, 128)] = high
-        rows_x[:, pl.ds(2 * N + turn * 128, 128)] = low
-
-    cos = jnp.dot(rows_x[...], first_cos[...], preferred_element_type=F32)
-    sin = jnp.dot(rows_x[...], first_sin[...], preferred_element_type=F32)
-    real = (cos[:288] - sin[288:]).reshape(4, 3, 24, M)
-    imag = (sin[:288] + cos[288:]).reshape(4, 3, 24, M)
-    for b in range(4):
-        for a in range(3):
-            out[0, a * 4 + b] = real[b, a]
-            out[1, a * 4 + b] = imag[b, a]
-
-    for turn in range(ROUNDS):
-
-        @pl.loop(1, COLS)
-        def _(k):
-            send_z(turn, lax.rem(gy + k, COLS), gy).wait_send()
-
-        @pl.loop(1, ROWS)
-        def _(k):
-            send_y(turn, lax.rem(gx + k, ROWS), gx).wait_send()
-
-
-    @pl.loop(1, DEVICES)
-    def _(k):
-        send_piece(lax.rem(me + k, DEVICES), me).wait_send()
+        for q in range(3):
+            stage_z(turn, q)
+            if turn == 0:
+                send_z(turn, q)
+        if turn == 1:
+            send_z(turn, 0)
+    for a in range(3):
+        send_z(2, a)
+
+    everything = pl.ds(0, 3)
+    for q in range(3):
+        wait_z(0, q)
+    stage_y(0, everything)
+    send_y(0, everything)
+    wait_z(1, 0)
+    stage_y(1, everything)
+    send_y(1, everything)
+    wait_y(0, everything)
+    cos, sin = stage_x(0, everything)
+    sum_cos[...] = cos
+    sum_sin[...] = sin
+    for a in range(3):
+        wait_z(2, a)
+        stage_y(2, pl.ds(a, 1))
+        send_y(2, pl.ds(a, 1))
+        if a == 0:
+            wait_y(1, everything)
+            cos, sin = stage_x(1, everything)
+            sum_cos[...] += cos
+            sum_sin[...] += sin
+
+    arrival(outbox.at[pl.ds(0, DEVICES - 1)], p_send)
+    arrival(in_y.at[:, pl.ds(0, COLS - 1)], z_send)
+
+    for a in range(3):
+        wait_y(2, pl.ds(a, 1))
+        cos, sin = stage_x(2, pl.ds(a, 1))
+        cos = cos + sum_cos[pl.ds(a * 192, 192), :]
+        sin = sin + sum_sin[pl.ds(a * 192, 192), :]
+        out[0, pl.ds(a * 4, 4)] = (cos[:96] - sin[96:]).reshape(4, 24, M)
+        out[1, pl.ds(a * 4, 4)] = (sin[:96] + cos[96:]).reshape(4, 24, M)
+    arrival(in_x.at[:, pl.ds(0, ROWS - 1)], y_send)
 
 
 def whole(owners, tile_ids, samples, kernel, offsets, third, second, first_cos, first_sin):
     operands = (owners, tile_ids, samples, kernel, offsets, third, second, first_cos, first_sin)
-    held = [pltpu.VMEM(x.shape, x.dtype) for x in operands]
+    held = [pltpu.VMEM(x.shape, x.dtype) for x in operands[:5]] + [
+        pltpu.VMEM((N, 3 * N), BF16),
+        pltpu.VMEM((N, 3 * N), BF16),
+        pltpu.VMEM((ROUNDS, N, M), BF16),
+        pltpu.VMEM((ROUNDS, N, M), BF16),
+    ]
     return pl.pallas_call(
         whole_kernel,
         out_shape=jax.ShapeDtypeStruct((2, 12, 24, M), F32),
@@ -423,28 +470,29 @@
             pltpu.VMEM((DEVICES, SLOT_ROWS, 128), F32),
             pltpu.VMEM((128, 128), F32),
             pltpu.VMEM((512, 1024), BF16),
-            pltpu.VMEM((2, 6, N, 128), BF16),
+            pltpu.VMEM((2, N, 256), BF16),
             pltpu.VMEM((ROUNDS, 8, 2, 9, 8, 128), F32),
             pltpu.VMEM((ROUNDS, COLS, 9, 8, 128), F32),
             pltpu.VMEM((N, 3 * N), BF16),
             pltpu.VMEM((ROUNDS, ROWS, 3, 24, 128), F32),
             pltpu.VMEM((ROUNDS, ROWS, 3, 24, 128), F32),
-            pltpu.VMEM((576, 3 * N), BF16),
-            pltpu.SemaphoreType.DMA((len(operands),)),
+            pltpu.VMEM((576, M), F32),
+            pltpu.VMEM((576, M), F32),
+            pltpu.SemaphoreType.REGULAR,
+            pltpu.SemaphoreType.DMA((13,)),
             pltpu.SemaphoreType.DMA,
-            pltpu.SemaphoreType.DMA((DEVICES,)),
-            pltpu.SemaphoreType.DMA((DEVICES,)),
-            pltpu.SemaphoreType.DMA((ROUNDS, COLS)),
-            pltpu.SemaphoreType.DMA((ROUNDS, COLS)),
-            pltpu.SemaphoreType.DMA((ROUNDS, ROWS)),
-            pltpu.SemaphoreType.DMA((ROUNDS, ROWS)),
-            pltpu.SemaphoreType.DMA((2, ROUNDS)),
+            pltpu.SemaphoreType.DMA,
+            pltpu.SemaphoreType.DMA((ROWS,)),
+            pltpu.SemaphoreType.DMA,
+            pltpu.SemaphoreType.DMA((3 * ROUNDS,)),
+            pltpu.SemaphoreType.DMA,
+            pltpu.SemaphoreType.DMA((3 * ROUNDS,)),
         ],
         compiler_params=pltpu.CompilerParams(
-            collective_id=0, has_side_effects=True, vmem_limit_bytes=62 << 20
+            collective_id=0, has_side_effects=True, vmem_limit_bytes=48 << 20
         ),
         name="whole",
-    )(*operands)
+    )(*[pltpu.with_memory_space_constraint(x, pltpu.HBM) for x in operands])
 
 
 def solution(mesh):

time: 71.8 us -> 63.1 us (0.88)
  Pallas kernels: 69.5 us -> 61.9 us
  other arithmetic: 2.08 us -> 1.01 us
    pallas_call x1, Pallas kernels: 69.5 us -> 61.9 us  [whole(): pl.pallas_call(whole_kernel, out_shape=jax.ShapeDtypeStruct((2, 12, 24, M...]
    mul x1, other arithmetic: 2.08 us -> 1.01 us  [on_device(): along_x * deapod_third[None, :, None, None]]
where the time goes in v4:
time: 63.1 us; the launch traced here: 63 us
  Pallas kernels  61.9 us (98%)
  other arithmetic  1.01 us (2%)
    pallas_call x1, Pallas kernels, whole(): pl.pallas_call(whole_kernel, out_shape=jax.ShapeDtypeStruct((2, 12, 24, M...  61.9 us

profile of v4, /device:TPU:1, one launch (start us, length us, event | category | flops | bytes accessed | tf_op | source)
XLA Modules:
  0.0 63.0 jit_solution(10714364787458749000)
XLA Ops:
  0.0 0.0 copy-start
  0.0 0.0 copy-start.1
  0.0 0.0 copy-start.2
  0.0 61.9 %whole.1 = f32[2,12,24,192]{3,2,1,0:T(8,128)S(1)} custom-call(s32[1,128]{1,0:T(1,128)} %bitcast.4, s32[1,128]{1,0:T(1,128)} %bitcast.5, f32[128,2,128]{2,1,0:T(2,128)} %samples_in.1, f32[128,3,4,128]{3,2,1,0:T(4,128)} %kernel_in.1, s32[3,128,128]{2,1,0:T(8,128)} %bitcast.3, bf16[384,768]{1,0:T(8,128)(2,1)} %constant.8.clone.third_in, ...), custom_call_target="tpu_custom_call" | custom-call | tf_op jit(solution)/shard_map/whole/pallas_call | solution.py:458
  61.9 0.0 copy-done
  61.9 0.0 copy-done.1
  62.0 0.0 copy-done.2
  62.0 1.0 %multiply_multiply_fusion = f32[2,12,24,192]{3,2,1,0:T(8,128)} fusion(f32[2,12,24,192]{3,2,1,0:T(8,128)S(1)} %whole.1, f32[192]{0:T(256)S(1)} %copy-done, f32[24]{0:T(128)S(1)} %copy-done.1, f32[12]{0:T(128)S(1)} %copy-done.2), kind=kLoop, calls=%fused_computation | loop fusion | flops 331776 | bytes 885648 | tf_op jit(solution)/shard_map/mul | solution.py:514
Async XLA Ops:
  0.0 61.9 %copy-start = (f32[192]{0:T(256)S(1)}, f32[192]{0:T(256)}, u32[]{:S(2)}) copy-start(f32[192]{0:T(256)} %param.17) | copy-start | bytes 2308
  0.0 61.9 %copy-start.1 = (f32[24]{0:T(128)S(1)}, f32[24]{0:T(128)}, u32[]{:S(2)}) copy-start(f32[24]{0:T(128)} %param.18) | copy-start | bytes 292
  0.0 62.0 %copy-start.2 = (f32[12]{0:T(128)S(1)}, f32[12]{0:T(128)}, u32[]{:S(2)}) copy-start(f32[12]{0:T(128)} %param.19) | copy-start | bytes 148

commit v5 on v4

--- a/solution.py
+++ b/solution.py
@@ -289,11 +289,11 @@
     def tile_at(turn, q, a):
         return q * 3 + a if turn == 0 else a * 3 + q
 
-    def part(turn, third_of):
-        return pl.ds(0, 9) if turn == 1 else pl.ds(3 * third_of, 3)
+    def part(third_of):
+        return pl.ds(3 * third_of, 3)
 
     def send_z(turn, third_of):
-        tiles_of = part(turn, third_of)
+        tiles_of = part(third_of)
         count = turn * 3 + third_of
 
         @pl.loop(1, COLS)
@@ -313,7 +313,7 @@
         ).start()
 
     def wait_z(turn, third_of):
-        arrival(in_y.at[turn, :, part(turn, third_of)], z_recv.at[turn * 3 + third_of])
+        arrival(in_y.at[turn, :, part(third_of)], z_recv.at[turn * 3 + third_of])
 
     def send_y(turn, thirds):
         count = turn * 3 + thirds.start
@@ -340,8 +340,8 @@
     row = lax.broadcasted_iota(jnp.int32, (24, 8, 128), 1)
     tile_of = lax.broadcasted_iota(jnp.int32, (48, 128), 0)
 
-    def stage_z(turn, q):
-        bases = [((2 * turn + r) * 3 + q) * 48 for r in range(2)]
+    def add_pieces(turn, columns):
+        bases = [((2 * turn + r) * 3 + q) * 48 for q in columns for r in range(2)]
         hits = [
             jnp.concatenate(
                 [jnp.where((tile_of + base).astype(F32) == tile_row, 1.0, 0.0) for base in bases], axis=0
@@ -353,11 +353,13 @@
             added = jnp.dot(hits, arrived[:, pl.ds(pair * 256, 256)], preferred_element_type=F32)
             for half, value in enumerate(split(added)):
                 for l in range(2):
-                    for r in range(2):
-                        cells[half, pl.ds((2 * pair + l) * 48, 48), pl.ds(r * 128, 128)] = value[
-                            r * 48 : r * 48 + 48, l * 128 : l * 128 + 128
-                        ]
-        high, low = cells[0], cells[1]
+                    for i in range(len(bases)):
+                        cells[columns[i // 2], half, pl.ds((2 * pair + l) * 48, 48), pl.ds(i % 2 * 128, 128)] = (
+                            value[i * 48 : i * 48 + 48, l * 128 : l * 128 + 128]
+                        )
+
+    def stage_z(turn, q):
+        high, low = cells[q, 0], cells[q, 1]
         product = jnp.dot(
             third[...], jnp.concatenate((high, high, low), axis=0), preferred_element_type=F32
         )
@@ -369,25 +371,23 @@
             out_z[turn, :, 0, tile_at(turn, q, a)] = even[a * 8 : a * 8 + 8]
             out_z[turn, :, 1, tile_at(turn, q, a)] = odd[a * 8 : a * 8 + 8]
 
-    def stage_y(turn, thirds):
-        for a in range(thirds.start, thirds.start + thirds.size):
+    def stage_y(parts):
+        for i, (turn, a) in enumerate(parts):
             for q in range(3):
                 value = in_y[turn, :, tile_at(turn, q, a)]
                 for bit in range(4):
                     value = exchange_bit(value, 1 << bit, 3 + bit)
                 high, low = split(value.reshape(128, 128))
-                rows_y[pl.ds(a * 128, 128), pl.ds(q * 128, 128)] = high
-                rows_y[pl.ds(a * 128, 128), pl.ds(N + q * 128, 128)] = high
-                rows_y[pl.ds(a * 128, 128), pl.ds(2 * N + q * 128, 128)] = low
+                rows_y[pl.ds(i * 128, 128), pl.ds(q * 128, 128)] = high
+                rows_y[pl.ds(i * 128, 128), pl.ds(N + q * 128, 128)] = high
+                rows_y[pl.ds(i * 128, 128), pl.ds(2 * N + q * 128, 128)] = low
         product = lax.dot_general(
-            second[...],
-            rows_y[pl.ds(thirds.start * 128, thirds.size * 128), :],
-            NT,
-            preferred_element_type=F32,
+            second[...], rows_y[pl.ds(0, len(parts) * 128), :], NT, preferred_element_type=F32
         )
-        for a in range(thirds.size):
-            done = combine(product[:, a * 128 : a * 128 + 128])
-            out_y[turn, :, thirds.start + a] = done.reshape(ROWS, 24, 128)
+        for i, (turn, a) in enumerate(parts):
+            done = combine(product[:, i * 128 : i * 128 + 128])
+            out_y[turn, :, a] = done.reshape(ROWS, 24, 128)
+            send_y(turn, pl.ds(a, 1))
 
     def stage_x(turn, thirds):
         values = []
@@ -402,37 +402,44 @@
             jnp.dot(rows, table[turn], preferred_element_type=F32) for table in (first_cos, first_sin)
         ]
 
-    for turn in range(ROUNDS):
-        for q in range(3):
-            stage_z(turn, q)
-            if turn == 0:
-                send_z(turn, q)
-        if turn == 1:
-            send_z(turn, 0)
-    for a in range(3):
-        send_z(2, a)
-
-    everything = pl.ds(0, 3)
+    def add_x(turn):
+        for a in range(3):
+            wait_y(turn, pl.ds(a, 1))
+        return stage_x(turn, pl.ds(0, 3))
+
+    for q in range(3):
+        add_pieces(0, (q,))
+        stage_z(0, q)
+        send_z(0, q)
+    add_pieces(1, (0, 1, 2))
+    for q in range(3):
+        stage_z(1, q)
+    send_z(1, 0)
+    send_z(1, 1)
+    add_pieces(2, (0, 1, 2))
+    for q in range(3):
+        stage_z(2, q)
+    send_z(1, 2)
     for q in range(3):
         wait_z(0, q)
-    stage_y(0, everything)
-    send_y(0, everything)
+    stage_y(((0, 0), (0, 1)))
+    send_z(2, 0)
     wait_z(1, 0)
-    stage_y(1, everything)
-    send_y(1, everything)
-    wait_y(0, everything)
-    cos, sin = stage_x(0, everything)
-    sum_cos[...] = cos
-    sum_sin[...] = sin
-    for a in range(3):
-        wait_z(2, a)
-        stage_y(2, pl.ds(a, 1))
-        send_y(2, pl.ds(a, 1))
-        if a == 0:
-            wait_y(1, everything)
-            cos, sin = stage_x(1, everything)
-            sum_cos[...] += cos
-            sum_sin[...] += sin
+    stage_y(((0, 2), (1, 0)))
+    send_z(2, 1)
+    wait_z(1, 1)
+    wait_z(1, 2)
+    stage_y(((1, 1), (1, 2)))
+    send_z(2, 2)
+    sum_cos[...], sum_sin[...] = add_x(0)
+    wait_z(2, 0)
+    wait_z(2, 1)
+    stage_y(((2, 0), (2, 1)))
+    cos, sin = add_x(1)
+    sum_cos[...] += cos
+    sum_sin[...] += sin
+    wait_z(2, 2)
+    stage_y(((2, 2),))
 
     arrival(outbox.at[pl.ds(0, DEVICES - 1)], p_send)
     arrival(in_y.at[:, pl.ds(0, COLS - 1)], z_send)
@@ -470,10 +477,10 @@
             pltpu.VMEM((DEVICES, SLOT_ROWS, 128), F32),
             pltpu.VMEM((128, 128), F32),
             pltpu.VMEM((512, 1024), BF16),
-            pltpu.VMEM((2, N, 256), BF16),
+            pltpu.VMEM((3, 2, N, 256), BF16),
             pltpu.VMEM((ROUNDS, 8, 2, 9, 8, 128), F32),
             pltpu.VMEM((ROUNDS, COLS, 9, 8, 128), F32),
-            pltpu.VMEM((N, 3 * N), BF16),
+            pltpu.VMEM((256, 3 * N), BF16),
             pltpu.VMEM((ROUNDS, ROWS, 3, 24, 128), F32),
             pltpu.VMEM((ROUNDS, ROWS, 3, 24, 128), F32),
             pltpu.VMEM((576, M), F32),

time: 63.1 us -> 60.4 us (0.957)
  Pallas kernels: 61.9 us -> 59.2 us
    pallas_call x1, Pallas kernels: 61.9 us -> 59.2 us  [whole(): pl.pallas_call(whole_kernel, out_shape=jax.ShapeDtypeStruct((2, 12, 24, M...]
where the time goes in v5:
time: 60.4 us; the launch traced here: 60.3 us
  Pallas kernels  59.2 us (98%)
  other arithmetic  1.01 us (2%)
    pallas_call x1, Pallas kernels, whole(): pl.pallas_call(whole_kernel, out_shape=jax.ShapeDtypeStruct((2, 12, 24, M...  59.2 us

profile of v5, /device:TPU:1, one launch (start us, length us, event | category | flops | bytes accessed | tf_op | source)
XLA Modules:
  0.0 60.3 jit_solution(7637054115086056788)
XLA Ops:
  0.0 0.0 copy-start
  0.0 0.0 copy-start.1
  0.0 0.0 copy-start.2
  0.0 59.2 %whole.1 = f32[2,12,24,192]{3,2,1,0:T(8,128)S(1)} custom-call(s32[1,128]{1,0:T(1,128)} %bitcast.4, s32[1,128]{1,0:T(1,128)} %bitcast.5, f32[128,2,128]{2,1,0:T(2,128)} %samples_in.1, f32[128,3,4,128]{3,2,1,0:T(4,128)} %kernel_in.1, s32[3,128,128]{2,1,0:T(8,128)} %bitcast.3, bf16[384,768]{1,0:T(8,128)(2,1)} %constant.8.clone.third_in, ...), custom_call_target="tpu_custom_call" | custom-call | tf_op jit(solution)/shard_map/whole/pallas_call | solution.py:465
  59.2 0.0 copy-done
  59.3 0.0 copy-done.1
  59.3 0.0 copy-done.2
  59.3 1.0 %multiply_multiply_fusion = f32[2,12,24,192]{3,2,1,0:T(8,128)} fusion(f32[2,12,24,192]{3,2,1,0:T(8,128)S(1)} %whole.1, f32[192]{0:T(256)S(1)} %copy-done, f32[24]{0:T(128)S(1)} %copy-done.1, f32[12]{0:T(128)S(1)} %copy-done.2), kind=kLoop, calls=%fused_computation | loop fusion | flops 331776 | bytes 885648 | tf_op jit(solution)/shard_map/mul | solution.py:521
Async XLA Ops:
  0.0 59.2 %copy-start = (f32[192]{0:T(256)S(1)}, f32[192]{0:T(256)}, u32[]{:S(2)}) copy-start(f32[192]{0:T(256)} %param.17) | copy-start | bytes 2308
  0.0 59.3 %copy-start.1 = (f32[24]{0:T(128)S(1)}, f32[24]{0:T(128)}, u32[]{:S(2)}) copy-start(f32[24]{0:T(128)} %param.18) | copy-start | bytes 292
  0.0 59.3 %copy-start.2 = (f32[12]{0:T(128)S(1)}, f32[12]{0:T(128)}, u32[]{:S(2)}) copy-start(f32[12]{0:T(128)} %param.19) | copy-start | bytes 148

commit v6 on v5

--- a/solution.py
+++ b/solution.py
@@ -164,16 +164,16 @@
     def greet(semaphore, x, y):
         pl.semaphore_signal(semaphore, inc=1, device_id=(x, y), device_id_type=MESH)
 
-    @pl.loop(1, COLS)
-    def _(k):
-        greet(barrier, gx, lax.rem(gy + k, COLS))
-
-    @pl.loop(1, ROWS)
-    def _(k):
-        greet(barrier, lax.rem(gx + k, ROWS), gy)
-
-    for load in loads[5:]:
-        load.start()
+    def in_column(k):
+        return jnp.where(gy + k >= COLS, gy + k - COLS, gy + k)
+
+    def in_row(k):
+        return jnp.where(gx + k >= ROWS, gx + k - ROWS, gx + k)
+
+    for k in range(1, COLS):
+        greet(barrier, gx, in_column(k))
+    for k in range(1, ROWS):
+        greet(barrier, in_row(k), gy)
 
     loads[0].wait()
     loads[1].wait()
@@ -202,9 +202,9 @@
     cell = lax.broadcasted_iota(jnp.int32, (8, 128), 0)
 
     def spread(step):
-        starts = [offsets[dim, pl.ds(pl.multiple_of(step * 16, 16), 16), :] for dim in range(3)]
-        for u in range(16):
-            n = step * 16 + u
+        starts = [offsets[dim, pl.ds(pl.multiple_of(step * 32, 32), 32), :] for dim in range(3)]
+        for u in range(32):
+            n = step * 32 + u
 
             placed = []
             for dim in range(3):
@@ -230,16 +230,12 @@
             both = lax.dot_general(left, right, NT, preferred_element_type=F32)
             pieces[n] = both[:8] + both[8:]
 
-    pl.loop(0, BLOCKS // 32)(spread)
+    pl.loop(0, BLOCKS // 64)(spread)
     pl.semaphore_wait(barrier, COLS + ROWS - 2)
-
-    @pl.loop(1, COLS)
-    def _(k):
-        greet(settled, gx, lax.rem(gy + k, COLS))
-
-    pl.loop(BLOCKS // 32, BLOCKS // 16)(spread)
+    for k in range(1, COLS):
+        greet(settled, gx, in_column(k))
+    pl.loop(BLOCKS // 64, BLOCKS // 32)(spread)
     place_slots.wait()
-    pl.semaphore_wait(settled, COLS - 1)
 
     def arrival(target, semaphore):
         pltpu.make_async_copy(target, target, semaphore).wait()
@@ -259,12 +255,29 @@
         outbox[peer, pl.ds(8, 8), :] = pieces[slots[1, peer]]
         outbox[peer, pl.ds(16, 1), :] = ids[pl.ds(peer // 64, 1), :]
 
-    @pl.loop(1, DEVICES)
-    def _(k):
-        peer = lax.rem(me + k, DEVICES)
+    def send_to(x, y):
+        peer = x * COLS + y
         fill(peer)
         send_piece(peer, me).start()
 
+    @pl.loop(1, COLS)
+    def _(k):
+        send_to(gx, in_column(k))
+
+    @pl.loop(1, ROWS)
+    def _(k):
+        send_to(in_row(k), gy)
+
+    pl.semaphore_wait(settled, COLS - 1)
+
+    @pl.loop(1, ROWS)
+    def _(i):
+        @pl.loop(1, COLS)
+        def _(k):
+            send_to(in_row(i), in_column(k))
+
+    for load in loads[5:]:
+        load.start()
     fill(me)
     pltpu.make_async_copy(outbox.at[me], inbox.at[me], p_recv.at[gx]).start()
 

time: 60.4 us -> 58.8 us (0.974)
  Pallas kernels: 59.2 us -> 57.6 us
    pallas_call x1, Pallas kernels: 59.2 us -> 57.6 us  [whole(): pl.pallas_call(whole_kernel, out_shape=jax.ShapeDtypeStruct((2, 12, 24, M...]
where the time goes in v6:
time: 58.8 us; the launch traced here: 58.6 us
  Pallas kernels  57.6 us (98%)
  other arithmetic  1.01 us (2%)
    pallas_call x1, Pallas kernels, whole(): pl.pallas_call(whole_kernel, out_shape=jax.ShapeDtypeStruct((2, 12, 24, M...  57.6 us

profile of v6, /device:TPU:1, one launch (start us, length us, event | category | flops | bytes accessed | tf_op | source)
XLA Modules:
  0.0 58.6 jit_solution(678083905017219071)
XLA Ops:
  0.0 0.0 copy-start
  0.0 0.0 copy-start.1
  0.0 0.0 copy-start.2
  0.0 57.6 %whole.1 = f32[2,12,24,192]{3,2,1,0:T(8,128)S(1)} custom-call(s32[1,128]{1,0:T(1,128)} %bitcast.4, s32[1,128]{1,0:T(1,128)} %bitcast.5, f32[128,2,128]{2,1,0:T(2,128)} %samples_in.1, f32[128,3,4,128]{3,2,1,0:T(4,128)} %kernel_in.1, s32[3,128,128]{2,1,0:T(8,128)} %bitcast.3, bf16[384,768]{1,0:T(8,128)(2,1)} %constant.8.clone.third_in, ...), custom_call_target="tpu_custom_call" | custom-call | tf_op jit(solution)/shard_map/whole/pallas_call | solution.py:478
  57.6 0.0 copy-done
  57.6 0.0 copy-done.1
  57.6 0.0 copy-done.2
  57.6 1.0 %multiply_multiply_fusion = f32[2,12,24,192]{3,2,1,0:T(8,128)} fusion(f32[2,12,24,192]{3,2,1,0:T(8,128)S(1)} %whole.1, f32[192]{0:T(256)S(1)} %copy-done, f32[24]{0:T(128)S(1)} %copy-done.1, f32[12]{0:T(128)S(1)} %copy-done.2), kind=kLoop, calls=%fused_computation | loop fusion | flops 331776 | bytes 885648 | tf_op jit(solution)/shard_map/mul | solution.py:534
Async XLA Ops:
  0.0 57.6 %copy-start = (f32[192]{0:T(256)S(1)}, f32[192]{0:T(256)}, u32[]{:S(2)}) copy-start(f32[192]{0:T(256)} %param.17) | copy-start | bytes 2308
  0.0 57.6 %copy-start.1 = (f32[24]{0:T(128)S(1)}, f32[24]{0:T(128)}, u32[]{:S(2)}) copy-start(f32[24]{0:T(128)} %param.18) | copy-start | bytes 292
  0.0 57.6 %copy-start.2 = (f32[12]{0:T(128)S(1)}, f32[12]{0:T(128)}, u32[]{:S(2)}) copy-start(f32[12]{0:T(128)} %param.19) | copy-start | bytes 148

commit v7 on v6

--- a/solution.py
+++ b/solution.py
@@ -98,6 +98,9 @@
     second_in,
     first_cos_in,
     first_sin_in,
+    scale_first_in,
+    scale_second_in,
+    scale_third_in,
     out,
     owners,
     tile_ids,
@@ -108,6 +111,9 @@
     second,
     first_cos,
     first_sin,
+    scale_first,
+    scale_second,
+    scale_third,
     pieces,
     ids,
     source_of,
@@ -154,6 +160,9 @@
                 (first_cos_in.at[:, pl.ds(0, 128)], first_cos.at[:, pl.ds(256, 128)]),
                 (first_sin_in, first_sin.at[:, pl.ds(0, 256)]),
                 (first_sin_in.at[:, pl.ds(0, 128)], first_sin.at[:, pl.ds(256, 128)]),
+                (scale_first_in, scale_first),
+                (scale_second_in, scale_second),
+                (scale_third_in, scale_third),
             )
         )
     ]
@@ -305,9 +314,9 @@
     def part(third_of):
         return pl.ds(3 * third_of, 3)
 
-    def send_z(turn, third_of):
-        tiles_of = part(third_of)
-        count = turn * 3 + third_of
+    def send_z(turn, third_of, single=None):
+        tiles_of = part(third_of) if single is None else pl.ds(3 * third_of + single, 1)
+        count = turn * 3 + third_of if single is None else 3 * ROUNDS + single
 
         @pl.loop(1, COLS)
         def _(k):
@@ -326,7 +335,11 @@
         ).start()
 
     def wait_z(turn, third_of):
-        arrival(in_y.at[turn, :, part(third_of)], z_recv.at[turn * 3 + third_of])
+        if turn == 0 and third_of == 0:
+            for single in range(3):
+                arrival(in_y.at[0, :, pl.ds(single, 1)], z_recv.at[3 * ROUNDS + single])
+        else:
+            arrival(in_y.at[turn, :, part(third_of)], z_recv.at[turn * 3 + third_of])
 
     def send_y(turn, thirds):
         count = turn * 3 + thirds.start
@@ -350,7 +363,6 @@
     def wait_y(turn, thirds):
         arrival(in_x.at[turn, :, thirds], y_recv.at[turn * 3 + thirds.start])
 
-    row = lax.broadcasted_iota(jnp.int32, (24, 8, 128), 1)
     tile_of = lax.broadcasted_iota(jnp.int32, (48, 128), 0)
 
     def add_pieces(turn, columns):
@@ -371,18 +383,31 @@
                             value[i * 48 : i * 48 + 48, l * 128 : l * 128 + 128]
                         )
 
+    def place_z(product, turn, q, thirds):
+        count = 8 * len(thirds)
+        near = combine(product[:, :128]).reshape(count, 8, 128)
+        far = combine(product[:, 128:]).reshape(count, 8, 128)
+        row = lax.broadcasted_iota(jnp.int32, (count, 8, 128), 1)
+        even = jnp.where(row < 4, near, pltpu.roll(far, 4, 1))
+        odd = jnp.where(row < 4, pltpu.roll(near, 4, 1), far)
+        for i, a in enumerate(thirds):
+            out_z[turn, :, 0, tile_at(turn, q, a)] = even[i * 8 : i * 8 + 8]
+            out_z[turn, :, 1, tile_at(turn, q, a)] = odd[i * 8 : i * 8 + 8]
+
     def stage_z(turn, q):
         high, low = cells[q, 0], cells[q, 1]
         product = jnp.dot(
             third[...], jnp.concatenate((high, high, low), axis=0), preferred_element_type=F32
         )
-        near = combine(product[:, :128]).reshape(24, 8, 128)
-        far = combine(product[:, 128:]).reshape(24, 8, 128)
-        even = jnp.where(row < 4, near, pltpu.roll(far, 4, 1))
-        odd = jnp.where(row < 4, pltpu.roll(near, 4, 1), far)
+        place_z(product, turn, q, range(3))
+
+    def first_stage_z():
+        high, low = cells[0, 0], cells[0, 1]
+        right = jnp.concatenate((high, high, low), axis=0)
         for a in range(3):
-            out_z[turn, :, 0, tile_at(turn, q, a)] = even[a * 8 : a * 8 + 8]
-            out_z[turn, :, 1, tile_at(turn, q, a)] = odd[a * 8 : a * 8 + 8]
+            left = jnp.concatenate((third[pl.ds(64 * a, 64), :], third[pl.ds(M + 64 * a, 64), :]), axis=0)
+            place_z(jnp.dot(left, right, preferred_element_type=F32), 0, 0, (a,))
+            send_z(0, 0, a)
 
     def stage_y(parts):
         for i, (turn, a) in enumerate(parts):
@@ -420,7 +445,9 @@
             wait_y(turn, pl.ds(a, 1))
         return stage_x(turn, pl.ds(0, 3))
 
-    for q in range(3):
+    add_pieces(0, (0,))
+    first_stage_z()
+    for q in range(1, 3):
         add_pieces(0, (q,))
         stage_z(0, q)
         send_z(0, q)
@@ -454,6 +481,10 @@
     wait_z(2, 2)
     stage_y(((2, 2),))
 
+    diagonal = lax.broadcasted_iota(jnp.int32, (24, 24), 0) == lax.broadcasted_iota(jnp.int32, (24, 24), 1)
+    column = jnp.sum(jnp.where(diagonal, scale_second[...], 0.0), axis=1, keepdims=True)
+    plane = column * scale_first[...]
+
     arrival(outbox.at[pl.ds(0, DEVICES - 1)], p_send)
     arrival(in_y.at[:, pl.ds(0, COLS - 1)], z_send)
 
@@ -462,18 +493,24 @@
         cos, sin = stage_x(2, pl.ds(a, 1))
         cos = cos + sum_cos[pl.ds(a * 192, 192), :]
         sin = sin + sum_sin[pl.ds(a * 192, 192), :]
-        out[0, pl.ds(a * 4, 4)] = (cos[:96] - sin[96:]).reshape(4, 24, M)
-        out[1, pl.ds(a * 4, 4)] = (sin[:96] + cos[96:]).reshape(4, 24, M)
+        real = (cos[:96] - sin[96:]).reshape(4, 24, M)
+        imag = (sin[:96] + cos[96:]).reshape(4, 24, M)
+        for b in range(4):
+            scale = plane * scale_third[0, a * 4 + b]
+            out[0, a * 4 + b] = real[b] * scale
+            out[1, a * 4 + b] = imag[b] * scale
     arrival(in_x.at[:, pl.ds(0, ROWS - 1)], y_send)
 
 
-def whole(owners, tile_ids, samples, kernel, offsets, third, second, first_cos, first_sin):
-    operands = (owners, tile_ids, samples, kernel, offsets, third, second, first_cos, first_sin)
+def whole(*operands):
     held = [pltpu.VMEM(x.shape, x.dtype) for x in operands[:5]] + [
         pltpu.VMEM((N, 3 * N), BF16),
         pltpu.VMEM((N, 3 * N), BF16),
         pltpu.VMEM((ROUNDS, N, M), BF16),
         pltpu.VMEM((ROUNDS, N, M), BF16),
+        pltpu.VMEM((1, M), F32),
+        pltpu.VMEM((1, 24), F32),
+        pltpu.SMEM((1, 12), F32),
     ]
     return pl.pallas_call(
         whole_kernel,
@@ -499,12 +536,12 @@
             pltpu.VMEM((576, M), F32),
             pltpu.VMEM((576, M), F32),
             pltpu.SemaphoreType.REGULAR,
-            pltpu.SemaphoreType.DMA((13,)),
+            pltpu.SemaphoreType.DMA((16,)),
             pltpu.SemaphoreType.DMA,
             pltpu.SemaphoreType.DMA,
             pltpu.SemaphoreType.DMA((ROWS,)),
             pltpu.SemaphoreType.DMA,
-            pltpu.SemaphoreType.DMA((3 * ROUNDS,)),
+            pltpu.SemaphoreType.DMA((3 * ROUNDS + 3,)),
             pltpu.SemaphoreType.DMA,
             pltpu.SemaphoreType.DMA((3 * ROUNDS,)),
         ],
@@ -519,7 +556,7 @@
     third, second, first_cos, first_sin = tables()
 
     def on_device(samples, kernel, offsets, owners, tile_ids, deapod_first, deapod_second, deapod_third):
-        along_x = whole(
+        return whole(
             owners.reshape(1, BLOCKS),
             tile_ids.reshape(1, BLOCKS),
             samples,
@@ -529,12 +566,9 @@
             second,
             first_cos,
             first_sin,
-        )
-        return (
-            along_x
-            * deapod_third[None, :, None, None]
-            * deapod_second[None, None, :, None]
-            * deapod_first[None, None, None, :]
+            deapod_first.reshape(1, M),
+            deapod_second.reshape(1, 24),
+            deapod_third.reshape(1, 12),
         )
 
     in_specs = (

time: 58.8 us -> 58.8 us (level)
  other arithmetic: 1.01 us -> 0 us
  local copies, waits for them, and re-layouts: 0.01 us -> 0.82 us
    mul x1 -> x0, other arithmetic: 1.01 us -> none  [on_device(): along_x * deapod_third[None, :, None, None]]
    unnamed x6 -> x1, local copies, waits for them, and re-layouts: 0.01 us -> 0.82 us
where the time goes in v7:
time: 58.8 us; the launch traced here: 58.7 us
  Pallas kernels  57.9 us (98%)
  local copies, waits for them, and re-layouts  0.82 us (1%)
    pallas_call x1, Pallas kernels, whole(): pl.pallas_call(whole_kernel, out_shape=jax.ShapeDtypeStruct((2, 12, 24, M...  57.9 us

profile of v7, /device:TPU:1, one launch (start us, length us, event | category | flops | bytes accessed | tf_op | source)
XLA Modules:
  0.0 58.7 jit_solution(6367798111825314193)
XLA Ops:
  0.0 57.9 %whole.1 = f32[2,12,24,192]{3,2,1,0:T(8,128)S(1)} custom-call(s32[1,128]{1,0:T(1,128)} %bitcast.8, s32[1,128]{1,0:T(1,128)} %bitcast.9, f32[128,2,128]{2,1,0:T(2,128)} %samples_in.1, f32[128,3,4,128]{3,2,1,0:T(4,128)} %kernel_in.1, s32[3,128,128]{2,1,0:T(8,128)} %bitcast.6, bf16[384,768]{1,0:T(8,128)(2,1)} %constant.8.clone.third_in, ...), custom_call_target="tpu_custom_call" | custom-call | tf_op jit(solution)/shard_map/whole/pallas_call | solution.py:515
  57.9 0.8 %copy.14 = f32[2,12,24,192]{3,2,1,0:T(8,128)} copy(f32[2,12,24,192]{3,2,1,0:T(8,128)S(1)} %whole.1) | data formatting | bytes 884736

commit v8 on v6

--- a/solution.py
+++ b/solution.py
@@ -230,11 +230,11 @@
             both = lax.dot_general(left, right, NT, preferred_element_type=F32)
             pieces[n] = both[:8] + both[8:]
 
-    pl.loop(0, BLOCKS // 64)(spread)
+    pl.loop(0, 1)(spread)
     pl.semaphore_wait(barrier, COLS + ROWS - 2)
     for k in range(1, COLS):
         greet(settled, gx, in_column(k))
-    pl.loop(BLOCKS // 64, BLOCKS // 32)(spread)
+    pl.loop(1, BLOCKS // 32)(spread)
     place_slots.wait()
 
     def arrival(target, semaphore):

time: 58.8 us -> 59 us (level)
  no operation moved by 1% of the time
where the time goes in v8:
time: 59 us; the launch traced here: 58.9 us
  Pallas kernels  57.8 us (98%)
  other arithmetic  1.01 us (2%)
    pallas_call x1, Pallas kernels, whole(): pl.pallas_call(whole_kernel, out_shape=jax.ShapeDtypeStruct((2, 12, 24, M...  57.8 us

profile of v8, /device:TPU:1, one launch (start us, length us, event | category | flops | bytes accessed | tf_op | source)
XLA Modules:
  0.0 58.9 jit_solution(6830786373916191967)
XLA Ops:
  0.0 0.0 copy-start
  0.0 0.0 copy-start.1
  0.0 0.0 copy-start.2
  0.0 57.8 %whole.1 = f32[2,12,24,192]{3,2,1,0:T(8,128)S(1)} custom-call(s32[1,128]{1,0:T(1,128)} %bitcast.4, s32[1,128]{1,0:T(1,128)} %bitcast.5, f32[128,2,128]{2,1,0:T(2,128)} %samples_in.1, f32[128,3,4,128]{3,2,1,0:T(4,128)} %kernel_in.1, s32[3,128,128]{2,1,0:T(8,128)} %bitcast.3, bf16[384,768]{1,0:T(8,128)(2,1)} %constant.8.clone.third_in, ...), custom_call_target="tpu_custom_call" | custom-call | tf_op jit(solution)/shard_map/whole/pallas_call | solution.py:478
  57.9 0.0 copy-done
  57.9 0.0 copy-done.1
  57.9 0.0 copy-done.2
  57.9 1.0 %multiply_multiply_fusion = f32[2,12,24,192]{3,2,1,0:T(8,128)} fusion(f32[2,12,24,192]{3,2,1,0:T(8,128)S(1)} %whole.1, f32[192]{0:T(256)S(1)} %copy-done, f32[24]{0:T(128)S(1)} %copy-done.1, f32[12]{0:T(128)S(1)} %copy-done.2), kind=kLoop, calls=%fused_computation | loop fusion | flops 331776 | bytes 885648 | tf_op jit(solution)/shard_map/mul | solution.py:534
Async XLA Ops:
  0.0 57.9 %copy-start = (f32[192]{0:T(256)S(1)}, f32[192]{0:T(256)}, u32[]{:S(2)}) copy-start(f32[192]{0:T(256)} %param.17) | copy-start | bytes 2308
  0.0 57.9 %copy-start.1 = (f32[24]{0:T(128)S(1)}, f32[24]{0:T(128)}, u32[]{:S(2)}) copy-start(f32[24]{0:T(128)} %param.18) | copy-start | bytes 292
  0.0 57.9 %copy-start.2 = (f32[12]{0:T(128)S(1)}, f32[12]{0:T(128)}, u32[]{:S(2)}) copy-start(f32[12]{0:T(128)} %param.19) | copy-start | bytes 148

commit v9 on v7

--- a/solution.py
+++ b/solution.py
@@ -314,9 +314,9 @@
     def part(third_of):
         return pl.ds(3 * third_of, 3)
 
-    def send_z(turn, third_of, single=None):
-        tiles_of = part(third_of) if single is None else pl.ds(3 * third_of + single, 1)
-        count = turn * 3 + third_of if single is None else 3 * ROUNDS + single
+    def send_z(turn, third_of):
+        tiles_of = part(third_of)
+        count = turn * 3 + third_of
 
         @pl.loop(1, COLS)
         def _(k):
@@ -335,11 +335,7 @@
         ).start()
 
     def wait_z(turn, third_of):
-        if turn == 0 and third_of == 0:
-            for single in range(3):
-                arrival(in_y.at[0, :, pl.ds(single, 1)], z_recv.at[3 * ROUNDS + single])
-        else:
-            arrival(in_y.at[turn, :, part(third_of)], z_recv.at[turn * 3 + third_of])
+        arrival(in_y.at[turn, :, part(third_of)], z_recv.at[turn * 3 + third_of])
 
     def send_y(turn, thirds):
         count = turn * 3 + thirds.start
@@ -401,14 +397,6 @@
         )
         place_z(product, turn, q, range(3))
 
-    def first_stage_z():
-        high, low = cells[0, 0], cells[0, 1]
-        right = jnp.concatenate((high, high, low), axis=0)
-        for a in range(3):
-            left = jnp.concatenate((third[pl.ds(64 * a, 64), :], third[pl.ds(M + 64 * a, 64), :]), axis=0)
-            place_z(jnp.dot(left, right, preferred_element_type=F32), 0, 0, (a,))
-            send_z(0, 0, a)
-
     def stage_y(parts):
         for i, (turn, a) in enumerate(parts):
             for q in range(3):
@@ -445,9 +433,7 @@
             wait_y(turn, pl.ds(a, 1))
         return stage_x(turn, pl.ds(0, 3))
 
-    add_pieces(0, (0,))
-    first_stage_z()
-    for q in range(1, 3):
+    for q in range(3):
         add_pieces(0, (q,))
         stage_z(0, q)
         send_z(0, q)
@@ -471,15 +457,15 @@
     wait_z(1, 2)
     stage_y(((1, 1), (1, 2)))
     send_z(2, 2)
-    sum_cos[...], sum_sin[...] = add_x(0)
     wait_z(2, 0)
     wait_z(2, 1)
     stage_y(((2, 0), (2, 1)))
+    wait_z(2, 2)
+    stage_y(((2, 2),))
+    sum_cos[...], sum_sin[...] = add_x(0)
     cos, sin = add_x(1)
     sum_cos[...] += cos
     sum_sin[...] += sin
-    wait_z(2, 2)
-    stage_y(((2, 2),))
 
     diagonal = lax.broadcasted_iota(jnp.int32, (24, 24), 0) == lax.broadcasted_iota(jnp.int32, (24, 24), 1)
     column = jnp.sum(jnp.where(diagonal, scale_second[...], 0.0), axis=1, keepdims=True)
@@ -541,7 +527,7 @@
             pltpu.SemaphoreType.DMA,
             pltpu.SemaphoreType.DMA((ROWS,)),
             pltpu.SemaphoreType.DMA,
-            pltpu.SemaphoreType.DMA((3 * ROUNDS + 3,)),
+            pltpu.SemaphoreType.DMA((3 * ROUNDS,)),
             pltpu.SemaphoreType.DMA,
             pltpu.SemaphoreType.DMA((3 * ROUNDS,)),
         ],

time: 58.8 us -> 58.5 us (level)
  no operation moved by 1% of the time
where the time goes in v9:
time: 58.5 us; the launch traced here: 58.3 us
  Pallas kernels  57.5 us (98%)
  local copies, waits for them, and re-layouts  0.82 us (1%)
    pallas_call x1, Pallas kernels, whole(): pl.pallas_call(whole_kernel, out_shape=jax.ShapeDtypeStruct((2, 12, 24, M...  57.5 us

profile of v9, /device:TPU:1, one launch (start us, length us, event | category | flops | bytes accessed | tf_op | source)
XLA Modules:
  0.0 58.3 jit_solution(15611536397181156959)
XLA Ops:
  0.0 57.5 %whole.1 = f32[2,12,24,192]{3,2,1,0:T(8,128)S(1)} custom-call(s32[1,128]{1,0:T(1,128)} %bitcast.8, s32[1,128]{1,0:T(1,128)} %bitcast.9, f32[128,2,128]{2,1,0:T(2,128)} %samples_in.1, f32[128,3,4,128]{3,2,1,0:T(4,128)} %kernel_in.1, s32[3,128,128]{2,1,0:T(8,128)} %bitcast.6, bf16[384,768]{1,0:T(8,128)(2,1)} %constant.8.clone.third_in, ...), custom_call_target="tpu_custom_call" | custom-call | tf_op jit(solution)/shard_map/whole/pallas_call | solution.py:501
  57.5 0.8 %copy.14 = f32[2,12,24,192]{3,2,1,0:T(8,128)} copy(f32[2,12,24,192]{3,2,1,0:T(8,128)S(1)} %whole.1) | data formatting | bytes 884736

commit v10 on v9

--- a/solution.py
+++ b/solution.py
@@ -318,9 +318,9 @@
         tiles_of = part(third_of)
         count = turn * 3 + third_of
 
-        @pl.loop(1, COLS)
+        @pl.loop(1, COLS, unroll=3)
         def _(k):
-            peer = lax.rem(gy + k, COLS)
+            peer = in_column(k)
             pltpu.make_async_remote_copy(
                 src_ref=out_z.at[turn, peer // 2, lax.rem(peer, 2), tiles_of],
                 dst_ref=in_y.at[turn, gy, tiles_of],
@@ -340,9 +340,9 @@
     def send_y(turn, thirds):
         count = turn * 3 + thirds.start
 
-        @pl.loop(1, ROWS)
+        @pl.loop(1, ROWS, unroll=7)
         def _(k):
-            peer = lax.rem(gx + k, ROWS)
+            peer = in_row(k)
             pltpu.make_async_remote_copy(
                 src_ref=out_y.at[turn, peer, thirds],
                 dst_ref=in_x.at[turn, gx, thirds],

time: 58.5 us -> 58.2 us (level)
  no operation moved by 1% of the time
where the time goes in v10:
time: 58.2 us; the launch traced here: 58.1 us
  Pallas kernels  57.3 us (98%)
  local copies, waits for them, and re-layouts  0.82 us (1%)
    pallas_call x1, Pallas kernels, whole(): pl.pallas_call(whole_kernel, out_shape=jax.ShapeDtypeStruct((2, 12, 24, M...  57.3 us

profile of v10, /device:TPU:1, one launch (start us, length us, event | category | flops | bytes accessed | tf_op | source)
XLA Modules:
  0.0 58.1 jit_solution(2993201775509452364)
XLA Ops:
  0.0 57.3 %whole.1 = f32[2,12,24,192]{3,2,1,0:T(8,128)S(1)} custom-call(s32[1,128]{1,0:T(1,128)} %bitcast.8, s32[1,128]{1,0:T(1,128)} %bitcast.9, f32[128,2,128]{2,1,0:T(2,128)} %samples_in.1, f32[128,3,4,128]{3,2,1,0:T(4,128)} %kernel_in.1, s32[3,128,128]{2,1,0:T(8,128)} %bitcast.6, bf16[384,768]{1,0:T(8,128)(2,1)} %constant.8.clone.third_in, ...), custom_call_target="tpu_custom_call" | custom-call | tf_op jit(solution)/shard_map/whole/pallas_call | solution.py:501
  57.3 0.8 %copy.14 = f32[2,12,24,192]{3,2,1,0:T(8,128)} copy(f32[2,12,24,192]{3,2,1,0:T(8,128)S(1)} %whole.1) | data formatting | bytes 884736
